TPU v7x, 768 devices: a whole 4x8x12 slice. The times are simulated.
768 devices in a mesh: dp: 192 (over z, y_hi, x, core), slab: 4 (over y_lo).
Axes of the slice: x: 4, y: 8 (y_hi: 2, y_lo: 4; y = y_hi * 4 + y_lo), z: 12, core: 2. Of those that a mesh axis runs over, the one named last changes fastest.
Arguments:
- gradient: bfloat16 [192, 3584, 1024], P('dp', 'slab'), may hold values from -500 to 500
Outputs:
- update: bfloat16 [192, 3584, 1024], P('dp', 'slab')
- grad_rms: float32 [], replicated
All inputs are finite; a program needn't handle non-finite values.
Results may differ from a plain program's by a relative error of at most 0.0034.
Values may be sent and summed in bfloat16 or wider, within the bound.
No kernel may reach another device: no remote copies, remote signals or barrier semaphores. Data moves between devices by JAX's collectives and lax.ppermute only.
A program may use at most 32 MiB of HBM per device.

v0:
```python
import math

import jax
import jax.numpy as jnp
from jax import lax
from jax.sharding import PartitionSpec as P

R = 3584


def square_sum(values):
    widened = values.astype(jnp.float32)
    return jnp.sum(widened * widened)


def polynomial(gram_part, product, factor):
    return (
        -4.775 * factor * gram_part.astype(jnp.float32) + 2.0315 * factor * factor * product
    ).astype(jnp.bfloat16)


def expert_step(slab_block):
    columns = slab_block
    product = lax.dot_general(
        columns, slab_block, (((0,), (0,)), ((), ())), preferred_element_type=jnp.float32
    )
    gram_part = lax.psum_scatter(
        product.astype(jnp.bfloat16).astype(jnp.bfloat16), "slab", scatter_dimension=0, tiled=True
    )
    portion = lax.all_gather(gram_part, "slab", axis=0, tiled=True)
    columns = gram_part
    product_sum = jnp.dot(columns, portion, preferred_element_type=jnp.float32)
    gram_squares = square_sum(portion)
    factor = 1.0 / (jnp.sqrt(gram_squares) + 1e-07)
    poly_part = polynomial(gram_part, product_sum, factor)
    columns = slab_block
    applied = jnp.dot(
        columns,
        lax.all_gather(poly_part, "slab", axis=0, tiled=True),
        preferred_element_type=jnp.float32,
    )
    scaled = math.sqrt(R) * jnp.sqrt(factor) * (3.4445 * slab_block.astype(jnp.float32) + applied)
    return scaled.astype(jnp.bfloat16)


def shards(gradient):
    local_squares = square_sum(gradient)
    grand_sum = lax.psum(local_squares, ("dp", "slab"))
    entries = gradient.size * lax.axis_size("dp") * lax.axis_size("slab")
    grad_rms = jnp.sqrt(grand_sum / entries)
    updates = [expert_step(gradient[0])]
    return (jnp.stack(updates, axis=0), grad_rms)


def solution(mesh):
    placed = (P("dp", "slab", None),)
    return jax.shard_map(
        shards, mesh=mesh, in_specs=placed, out_specs=(P("dp", "slab", None), P()), check_vma=False
    )
```

profile of v0, /device:TPU:56, one launch (start us, length us, event | category | flops | bytes accessed | tf_op | source)
XLA Modules:
  0.0 269.2 jit_solution(5979752754034421770)
XLA Ops:
  7.2 0.0 reduce-scatter.2.cloned.1.call-start
  7.2 5.8 %convolution_convert_fusion = bf16[1024,1024]{1,0:T(8,128)(2,1)} fusion(bf16[1,896,1024]{2,1,0:T(8,128)(2,1)} %param.1), kind=kOutput, calls=%fused_computation.5 | convolution fusion | flops 1880096768 | bytes 3932160 | tf_op jit(solution)/shard_map/dot_general | solution.py:24
  13.0 0.0 reduce-scatter.2.cloned.1.call-update
  13.0 0.0 all-gather.3.cloned.1.call-start
  13.1 61.3 %reduce-scatter.2.cloned.1.call-done = bf16[256,1024]{1,0:T(8,128)(2,1)} async-done(((bf16[1024,1024]{1,0:T(8,128)(2,1)}), bf16[256,1024]{1,0:T(8,128)(2,1)}) %reduce-scatter.2.cloned.1.call-update) | async-done | bytes 524304 | tf_op jit(solution)/shard_map/reduce_scatter | solution.py:27
  74.4 0.0 copy-start.1
  74.4 0.0 all-gather.3.cloned.1.call-update
  74.4 0.0 all-gather.5.cloned.1.call-start
  74.4 57.3 %all-gather.3.cloned.1.call-done = bf16[1024,1024]{1,0:T(8,128)(2,1)} async-done(((bf16[256,1024]{1,0:T(8,128)(2,1)}), bf16[1024,1024]{1,0:T(8,128)(2,1)}) %all-gather.3.cloned.1.call-update) | async-done | bytes 2097168 | tf_op jit(solution)/shard_map/all_gather | solution.py:30
  131.7 3.3 %multiply_reduce_fusion = f32[]{:T(128)} fusion(bf16[1024,1024]{1,0:T(8,128)(2,1)} %all-gather.3.cloned.1.call-done), kind=kLoop, calls=%fused_computation | loop fusion | flops 3145727 | bytes 2097156 | tf_op jit(solution)/shard_map/reduce_sum | solution.py:13
  135.7 0.0 copy-done.1
  135.7 0.0 copy-start
  135.7 3.2 %fusion.8 = bf16[256,1024]{1,0:T(8,128)(2,1)} fusion(bf16[256,1024]{1,0:T(8,128)(2,1)S(1)} %copy-done.1, bf16[1024,1024]{1,0:T(8,128)(2,1)} %all-gather.3.cloned.1.call-done, f32[]{:T(128)S(6)} %mul.39, f32[]{:T(128)S(6)} %mul_shard_map.10), kind=kOutput, calls=%fused_computation.11 | convolution fusion | flops 538181632 | bytes 3145736 | tf_op jit(solution)/shard_map/dot_general | solution.py:32
  139.0 0.0 all-gather.5.cloned.1.call-update
  139.0 0.0 copy-done
  139.0 1.5 multiply_reduce_fusion.1
  140.6 108.2 %psum.7 = f32[]{:T(128)} all-reduce(f32[]{:T(128)} %multiply_reduce_fusion.1), channel_id=1, replica_groups=mesh['dp'=192,'slab'=4] {'dp','slab'}, use_global_device_ids=true, to_apply=%region_3.0 | all-reduce | flops 1 | bytes 8 | tf_op jit(solution)/shard_map/psum | solution.py:48
  248.8 2.4 copy.3
  252.0 0.0 all-gather.5.cloned.1.call-done
  252.0 5.8 %fusion.4 = bf16[1,896,1024]{1,2,0:T(8,128)(2,1)} fusion(bf16[1024,1024]{1,0:T(8,128)(2,1)} %all-gather.5.cloned.1.call-done, bf16[1,896,1024]{2,1,0:T(8,128)(2,1)S(1)} %copy-done, bf16[1,896,1024]{1,2,0:T(8,128)(2,1)} %copy.3, f32[]{:T(128)S(6)} %mul_shard_map.9), kind=kOutput, calls=%fused_computation.8 | convolution fusion | flops 1883635712 | bytes 7602180 | tf_op jit(solution)/shard_map/dot_general | solution.py:37
  257.8 3.8 %copy.4 = bf16[1,896,1024]{2,1,0:T(8,128)(2,1)} copy(bf16[1,896,1024]{1,2,0:T(8,128)(2,1)} %fusion.4) | data formatting | bytes 3670016
Async XLA Ops:
  7.2 67.2 %reduce-scatter.2.cloned.1.call-start = ((), (), s32[]{:S(2)}) async-start(), calls=%async_computation.1 | async-start | bytes 2621440 | tf_op jit(solution)/shard_map/reduce_scatter | solution.py:27
  13.0 118.7 %all-gather.3.cloned.1.call-start = ((), (), s32[]{:S(2)}) async-start(), calls=%async_computation.2 | async-start | bytes 2621440 | tf_op jit(solution)/shard_map/all_gather | solution.py:30
  74.4 61.4 %copy-start.1 = (bf16[256,1024]{1,0:T(8,128)(2,1)S(1)}, bf16[256,1024]{1,0:T(8,128)(2,1)}, u32[]{:S(2)}) copy-start(bf16[256,1024]{1,0:T(8,128)(2,1)} %reduce-scatter.2.cloned.1.call-done) | copy-start | bytes 1572868
  74.4 177.6 %all-gather.5.cloned.1.call-start = ((), (), s32[]{:S(2)}) async-start(), calls=%async_computation.3 | async-start | bytes 2621440 | tf_op jit(solution)/shard_map/all_gather | solution.py:39
  135.7 3.3 %copy-start = (bf16[1,896,1024]{2,1,0:T(8,128)(2,1)S(1)}, bf16[1,896,1024]{2,1,0:T(8,128)(2,1)}, u32[]{:S(2)}) copy-start(bf16[1,896,1024]{2,1,0:T(8,128)(2,1)} %param.1) | copy-start | bytes 5505028
Sparse Core Ops, SparseCore 0:
  13.1 61.1 reduce-scatter.1
  76.8 54.9 all-gather.2
  139.1 55.2 all-gather.4
where the time goes:
time: 275 us; the launch traced here: 269 us
  waiting for transfers between devices  119 us (43%)
  blocking collectives  108 us (39%)
  between operations  16.4 us (6%)
  matrix products  14.8 us (5%)
  local copies, waits for them, and re-layouts  6.23 us (2%)
  other arithmetic  4.82 us (2%)
    psum x1, blocking collectives, shards(): grand_sum = lax.psum(local_squares, ('dp', 'slab'))  108 us
    reduce_scatter x1, waiting for transfers between devices, expert_step(): lax.psum_scatter(product.astype(jnp.bfloat16).astype(jnp.bfloat16), 'slab...  61.3 us
    all_gather x1, waiting for transfers between devices, expert_step(): portion = lax.all_gather(gram_part, 'slab', axis=0, tiled=True)  57.3 us
    unnamed x6, local copies, waits for them, and re-layouts  6.23 us
    dot_general x1, matrix products, expert_step(): jnp.dot(columns, lax.all_gather(poly_part, 'slab', axis=0, tiled=True), p...  5.81 us
    dot_general x1, matrix products, expert_step(): lax.dot_general(columns, slab_block, (((0,), (0,)), ((), ())), preferred_...  5.79 us
  transfers between devices with their start and end apart: 3, of which 2 were waited for; matrix products, arithmetic and copies ran while one was open for 1% of the time, Pallas kernels for 0%

commit v1 on v0

v1 whole, which is shorter than its diff:
```python
import functools
import math

import jax
import jax.numpy as jnp
from jax import lax
from jax.experimental import pallas as pl
from jax.experimental.pallas import tpu as pltpu
from jax.sharding import PartitionSpec as P

R = 3584
C = 1024
B = 256
H = 128
ROWS = 2 * B + 16

FULL = ((1, 0), (2, 1), (3, 2), (3, 0))
HALF = ((2, 0, 0), (2, 0, 1), (3, 1, 0), (3, 1, 1))


def pick(p, values):
    out = jnp.int32(values[0])
    for k in range(1, len(values)):
        out = jnp.where(p == k, jnp.int32(values[k]), out)
    return out


def lower(shape=(H, H)):
    rows = lax.broadcasted_iota(jnp.int32, shape, 0)
    cols = lax.broadcasted_iota(jnp.int32, shape, 1)
    return rows, cols


def columns(x_ref, start, width):
    return x_ref[0, :, pl.ds(pl.multiple_of(start, H), width)]


def outer(a, b):
    return lax.dot_general(a, b, (((0,), (0,)), ((), ())), preferred_element_type=jnp.float32)


def encode(total):
    hi = total.astype(jnp.bfloat16)
    rest = total - hi.astype(jnp.float32)
    mid = rest.astype(jnp.bfloat16)
    low = (rest - mid.astype(jnp.float32)).astype(jnp.bfloat16)
    return hi, mid, low


def decode(extras):
    wide = extras.astype(jnp.float32)
    return wide[1:2, :] + wide[2:3, :] + wide[3:4, :]


def extras_of(diagonal, total):
    hi, mid, low = encode(total)
    row = lax.broadcasted_iota(jnp.int32, (16, B), 0)
    out = jnp.where(row == 0, diagonal, 0.0)
    for k, part in ((1, hi), (2, mid), (3, low)):
        out = jnp.where(row == k, part.astype(jnp.float32), out)
    return out.astype(jnp.bfloat16)


def quarter(x_ref, p, total, out_ref):
    own = columns(x_ref, p * B, B)
    diag = outer(own, own)
    fi, fj = (pick(p, [f[k] for f in FULL]) for k in (0, 1))
    out_ref[0:B, :] = outer(columns(x_ref, fi * B, B), columns(x_ref, fj * B, B)).astype(jnp.bfloat16)
    hi, hj, part = (pick(p, [h[k] for h in HALF]) for k in (0, 1, 2))
    out_ref[B : B + H, :] = outer(
        columns(x_ref, hi * B + part * H, H), columns(x_ref, hj * B, B)
    ).astype(jnp.bfloat16)
    rows, cols = lower()
    first, last = diag[:H, :H], diag[H:, H:]
    out_ref[B + H : 2 * B, :H] = diag[H:, :H].astype(jnp.bfloat16)
    out_ref[B + H : 2 * B, H:] = jnp.where(rows > cols, first, last).astype(jnp.bfloat16)
    line = jnp.sum(jnp.where(rows == cols, first, 0.0), axis=0, keepdims=True)
    out_ref[2 * B :, :] = extras_of(jnp.concatenate([line, line], axis=1), total)


def first_kernel(own_ref, x_ref, out_ref, sum_ref):
    wide = x_ref[0].astype(jnp.float32)
    squares = jnp.sum(wide * wide, axis=0, keepdims=True)
    total = jnp.sum(squares, axis=1, keepdims=True)
    total = jnp.broadcast_to(total, (1, B))
    sum_ref[...] = jnp.broadcast_to(total[:, :H], (8, H))
    quarter(x_ref, 2 * (1 - own_ref[0]), total, out_ref)


def second_kernel(own_ref, x_ref, sum_ref, send_ref, keep0_ref, keep1_ref):
    own = own_ref[0]
    total = jnp.broadcast_to(sum_ref[0:1, 0:1], (1, B))
    quarter(x_ref, 2 * (1 - own) + 1, total, send_ref)
    quarter(x_ref, 2 * own, total, keep0_ref)
    quarter(x_ref, 2 * own + 1, total, keep1_ref)


def add_kernel(a_ref, b_ref, out_ref, sum_ref):
    body = slice(0, 2 * B)
    out_ref[body, :] = (a_ref[body, :].astype(jnp.float32) + b_ref[body, :].astype(jnp.float32)).astype(jnp.bfloat16)
    a, b = a_ref[2 * B :, :], b_ref[2 * B :, :]
    total = decode(a) + decode(b)
    out_ref[2 * B :, :] = extras_of(a[0:1, :].astype(jnp.float32) + b[0:1, :].astype(jnp.float32), total)
    sum_ref[...] = jnp.broadcast_to(total[:, :H], (8, H))


def final_kernel(own_ref, k0_ref, k1_ref, r0_ref, r1_ref, x_ref, out_ref, gram, poly, scale):
    @pl.when(pl.program_id(0) == 0)
    def _():
        mine = own_ref[0] == 0
        kept, received = (k0_ref, k1_ref), (r0_ref, r1_ref)
        rows, cols = lower()
        squares = jnp.zeros((H, B), jnp.float32)
        for p in range(4):
            keep, recv = kept[p % 2], received[p % 2]
            low = p < 2

            def get(part):
                k, r = keep[part, :], recv[part, :]
                return jnp.where(mine, k, r) if low else jnp.where(mine, r, k)

            def put(i, j, block):
                gram[i : i + block.shape[0], j : j + block.shape[1]] = block
                gram[j : j + block.shape[1], i : i + block.shape[0]] = block.T

            block = get(slice(0, B))
            fi, fj = FULL[p]
            put(fi * B, fj * B, block)
            wide = block.astype(jnp.float32)
            squares += 2.0 * (wide[:H] * wide[:H] + wide[H:] * wide[H:])
            block = get(slice(B, B + H))
            hi, hj, part = HALF[p]
            put(hi * B + part * H, hj * B, block)
            wide = block.astype(jnp.float32)
            squares += 2.0 * wide * wide
            block = get(slice(B + H, 2 * B))
            put(p * B + H, p * B, block[:, :H])
            fold = block[:, H:].astype(jnp.float32)
            flip = fold.T
            line = get(slice(2 * B, 2 * B + 16))[0:1, :H].astype(jnp.float32)
            upper = jnp.where(rows < cols, flip, jnp.where(rows == cols, jnp.broadcast_to(line, (H, H)), fold))
            second = jnp.where(rows > cols, flip, fold)
            gram[p * B : p * B + H, p * B : p * B + H] = upper.astype(jnp.bfloat16)
            gram[p * B + H : (p + 1) * B, p * B + H : (p + 1) * B] = second.astype(jnp.bfloat16)
            wide = block[:, :H].astype(jnp.float32)
            squares += jnp.concatenate([2.0 * wide * wide, upper * upper + second * second], axis=1)
        norm = jnp.sqrt(jnp.sum(jnp.sum(squares, axis=0, keepdims=True), axis=1, keepdims=True))
        factor = 1.0 / (norm + 1e-07)
        scale[...] = jnp.broadcast_to(math.sqrt(R) * jnp.sqrt(factor), (8, H))
        for i in range(4):
            for j in range(i + 1):
                product = jnp.dot(
                    gram[i * B : (i + 1) * B, :], gram[:, j * B : (j + 1) * B], preferred_element_type=jnp.float32
                )
                block = gram[i * B : (i + 1) * B, j * B : (j + 1) * B].astype(jnp.float32)
                block = (-4.775 * factor * block + 2.0315 * factor * factor * product).astype(jnp.bfloat16)
                poly[i * B : (i + 1) * B, j * B : (j + 1) * B] = block
                if i != j:
                    poly[j * B : (j + 1) * B, i * B : (i + 1) * B] = block.T

    x = x_ref[0]
    applied = jnp.dot(x, poly[...], preferred_element_type=jnp.float32)
    out_ref[0] = (scale[0:1, 0:1] * (3.4445 * x.astype(jnp.float32) + applied)).astype(jnp.bfloat16)


PIECE = jax.ShapeDtypeStruct((ROWS, B), jnp.bfloat16)
TILE = jax.ShapeDtypeStruct((8, H), jnp.float32)
SMEM = pl.BlockSpec(memory_space=pltpu.SMEM)
VMEM = pl.BlockSpec(memory_space=pltpu.VMEM)


def call(kernel, n_in, outs, flops, nbytes):
    return pl.pallas_call(
        kernel,
        out_shape=outs,
        in_specs=[SMEM] + [VMEM] * n_in,
        out_specs=[VMEM] * len(outs),
        cost_estimate=pl.CostEstimate(flops=flops, bytes_accessed=nbytes, transcendentals=0),
        compiler_params=pltpu.CompilerParams(vmem_limit_bytes=16 << 20),
    )


def add_pieces(a, b):
    return pl.pallas_call(
        add_kernel,
        out_shape=[PIECE, TILE],
        in_specs=[VMEM] * 2,
        out_specs=[VMEM] * 2,
        cost_estimate=pl.CostEstimate(flops=ROWS * B, bytes_accessed=6 * ROWS * B, transcendentals=0),
        compiler_params=pltpu.CompilerParams(vmem_limit_bytes=4 << 20),
    )(a, b)


def finish(own, k0, k1, r0, r1, x, rows):
    step = 128
    return pl.pallas_call(
        final_kernel,
        grid=(rows // step,),
        out_shape=jax.ShapeDtypeStruct((1, rows, C), jnp.bfloat16),
        in_specs=[SMEM] + [VMEM] * 4 + [pl.BlockSpec((1, step, C), lambda i: (0, i, 0))],
        out_specs=pl.BlockSpec((1, step, C), lambda i: (0, i, 0)),
        scratch_shapes=[
            pltpu.VMEM((C, C), jnp.bfloat16),
            pltpu.VMEM((C, C), jnp.bfloat16),
            pltpu.VMEM((8, H), jnp.float32),
        ],
        cost_estimate=pl.CostEstimate(flops=4 * rows * C * C, bytes_accessed=4 * rows * C, transcendentals=0),
        compiler_params=pltpu.CompilerParams(vmem_limit_bytes=24 << 20),
    )(own, k0, k1, r0, r1, x)


PAIR = [(0, 1), (1, 0), (2, 3), (3, 2)]
CROSS = [(1, 2), (2, 1), (0, 3), (3, 0)]
Z, YH, X, CORES = 12, 2, 4, 2


def moved(dz=0, flip=False, dx=0, other=False):
    pairs = []
    for z in range(Z):
        for yh in range(YH):
            for x in range(X):
                for c in range(CORES):
                    src = ((z * YH + yh) * X + x) * CORES + c
                    to = (((z + dz) % Z * YH + yh ^ flip) * X + (x + dx) % X) * CORES + (c ^ other)
                    pairs.append((src, to))
    return pairs


def spread(total):
    for shifts in (
        [moved(other=True)],
        [moved(dx=1)],
        [moved(dx=2)],
        [moved(dz=4), moved(dz=8)],
        [moved(dz=2)],
        [moved(dz=1)],
        [moved(flip=True)],
    ):
        total = functools.reduce(jnp.add, [lax.ppermute(total, "dp", s) for s in shifts], total)
    return total


def shards(gradient):
    rows = gradient.shape[1]
    place = lax.axis_index("slab")
    own = jnp.where((place == 1) | (place == 2), 1, 0).astype(jnp.int32).reshape(1)
    send0, tile = call(first_kernel, 1, [PIECE, TILE], rows * B * B * 5, 2 * rows * C)(own, gradient)
    got0 = lax.ppermute(send0, "slab", PAIR)
    send1, keep0, keep1 = call(second_kernel, 2, [PIECE] * 3, rows * B * B * 15, 2 * rows * C)(own, gradient, tile)
    got1 = lax.ppermute(send1, "slab", PAIR)
    half0, _ = add_pieces(keep0, got0)
    cross0 = lax.ppermute(half0, "slab", CROSS)
    half1, _ = add_pieces(keep1, got1)
    cross1 = lax.ppermute(half1, "slab", CROSS)
    whole0, total = add_pieces(half0, cross0)
    other0 = lax.ppermute(whole0, "slab", PAIR)
    whole1, _ = add_pieces(half1, cross1)
    other1 = lax.ppermute(whole1, "slab", PAIR)
    update = finish(own, whole0, whole1, other0, other1, gradient, rows)
    total = spread(total)
    entries = gradient.size * lax.axis_size("dp") * lax.axis_size("slab")
    return update, jnp.sqrt(total[0, 0] / entries)


def solution(mesh):
    return jax.shard_map(
        shards, mesh=mesh, in_specs=(P("dp", "slab", None),), out_specs=(P("dp", "slab", None), P()), check_vma=False
    )
```

time: 275 us -> 118 us (0.43); the launches traced: 269 us -> 118 us
  blocking collectives: 108 us -> 0 us
  waiting for transfers between devices: 119 us -> 34.7 us
  starting transfers between devices: 0.12 us -> 67.4 us
  matrix products: 14.8 us -> 0 us
  between operations: 16.4 us -> 2.66 us
  Pallas kernels: 0 us -> 10.9 us
  other arithmetic: 4.82 us -> 0.02 us
  local copies, waits for them, and re-layouts: 6.23 us -> 2.02 us
    psum x1 -> x0, blocking collectives: 108 us -> none  [shards(): grand_sum = lax.psum(local_squares, ('dp', 'slab'))]
    ppermute x0 -> x14, starting transfers between devices: none -> 67.4 us  [the longest x8 37 us: spread(): lax.ppermute(total, 'dp', s)]
    reduce_scatter x1 -> x0, waiting for transfers between devices: 61.3 us -> none  [expert_step(): lax.psum_scatter(product.astype(jnp.bfloat16).astype(jnp.bfloat16), 'slab...]
    all_gather x2 -> x0, waiting for transfers between devices: 57.3 us -> none  [the longest x1 57.3 us: expert_step(): portion = lax.all_gather(gram_part, 'slab', axis=0, tiled=True)]
    ppermute x0 -> x14, waiting for transfers between devices: none -> 34.7 us  [the longest x8 27.3 us: spread(): lax.ppermute(total, 'dp', s)]
    dot_general x3 -> x0, matrix products: 14.8 us -> none  [the longest x1 5.81 us: expert_step(): jnp.dot(columns, lax.all_gather(poly_part, 'slab', axis=0, tiled=True), p...]
    pallas_call x0 -> x7, Pallas kernels: none -> 10.9 us  [the longest x1 6.9 us: finish(): pl.pallas_call(final_kernel, grid=(rows // step,), out_shape=jax.ShapeDty...]
    reduce_sum x2 -> x0, other arithmetic: 4.82 us -> none  [square_sum(): return jnp.sum(widened * widened)]
  transfers between devices with their start and end apart: 3 -> 14, of which waited for: 2 -> 9; matrix products, arithmetic and copies ran while one was open for 1% -> 0% of each run, Pallas kernels for 0% -> 3%
where the time goes in v1:
time: 118 us
  starting transfers between devices  67.4 us (57%)
  waiting for transfers between devices  34.7 us (29%)
  Pallas kernels  10.9 us (9%)
  between operations  2.66 us (2%)
  local copies, waits for them, and re-layouts  2.02 us (2%)
    ppermute x8, starting transfers between devices, spread(): lax.ppermute(total, 'dp', s)  37 us
    ppermute x8, waiting for transfers between devices, spread(): lax.ppermute(total, 'dp', s)  27.3 us
    ppermute x1, starting transfers between devices, shards(): other0 = lax.ppermute(whole0, 'slab', PAIR)  12.2 us
    pallas_call x1, Pallas kernels, finish(): pl.pallas_call(final_kernel, grid=(rows // step,), out_shape=jax.ShapeDty...  6.9 us
    ppermute x1, starting transfers between devices, shards(): cross0 = lax.ppermute(half0, 'slab', CROSS)  4.81 us
    ppermute x1, starting transfers between devices, shards(): cross1 = lax.ppermute(half1, 'slab', CROSS)  4.03 us
    ppermute x1, waiting for transfers between devices, shards(): got0 = lax.ppermute(send0, 'slab', PAIR)  3.84 us
    ppermute x1, waiting for transfers between devices, shards(): cross0 = lax.ppermute(half0, 'slab', CROSS)  3.55 us
  transfers between devices with their start and end apart: 14, of which 9 were waited for; matrix products, arithmetic and copies ran while one was open for 0% of the time, Pallas kernels for 3%

profile of v1, /device:TPU:56, one launch (start us, length us, event | category | flops | bytes accessed | tf_op | source)
XLA Modules:
  0.0 117.8 jit_solution(12613046031585828606)
XLA Ops:
  0.6 0.0 copy-start
  0.7 1.5 %copy-done = bf16[1,896,1024]{2,1,0:T(8,128)(2,1)S(1)} copy-done((bf16[1,896,1024]{2,1,0:T(8,128)(2,1)S(1)}, bf16[1,896,1024]{2,1,0:T(8,128)(2,1)}, u32[]{:S(2)}) %copy-start) | copy-done | bytes 1835032
  2.1 0.7 shard_map.30
  2.8 3.3 %collective-permute-start = (bf16[528,256]{1,0:T(8,128)(2,1)S(1)}, bf16[528,256]{1,0:T(8,128)(2,1)S(1)}, u32[]{:S(2)}, u32[]{:S(2)}) collective-permute-start(bf16[528,256]{1,0:T(8,128)(2,1)S(1)} %get-tuple-element.14), channel_id=1, source_target_pairs={{0,1},{1,0},{2,3},{3,2},{4,5},{5,4},{6,7},{7,6},{8,9},{9,8},{10,11... | collective-permute-start | bytes 811016 | tf_op jit(solution)/shard_map/ppermute | solution.py:248
  6.1 1.4 %shard_map.31 = (bf16[528,256]{1,0:T(8,128)(2,1)S(1)}, bf16[528,256]{1,0:T(8,128)(2,1)S(1)}, bf16[528,256]{1,0:T(8,128)(2,1)S(1)}) custom-call(s32[1]{0:T(128)} %bitcast.own_ref, bf16[1,896,1024]{2,1,0:T(8,128)(2,1)S(1)} %copy-done, f32[8,128]{1,0:T(8,128)S(1)} %get-tuple-element.12.sum_ref), custom_call_target="tpu_custom_call" | custom-call | flops 880803840 | bytes 1835008 | tf_op jit(solution)/shard_map/pallas_call | solution.py:249
  7.5 0.0 copy-start.1
  7.5 2.7 %collective-permute-start.2 = (bf16[528,256]{1,0:T(8,128)(2,1)S(1)}, bf16[528,256]{1,0:T(8,128)(2,1)S(1)}, u32[]{:S(2)}, u32[]{:S(2)}) collective-permute-start(bf16[528,256]{1,0:T(8,128)(2,1)S(1)} %get-tuple-element.18), channel_id=1, source_target_pairs={{0,1},{1,0},{2,3},{3,2},{4,5},{5,4},{6,7},{7,6},{8,9},{9,8},{10,11... | collective-permute-start | bytes 811016 | tf_op jit(solution)/shard_map/ppermute | solution.py:250
  10.2 3.8 %collective-permute-done.b_ref = bf16[528,256]{1,0:T(8,128)(2,1)S(1)} collective-permute-done((bf16[528,256]{1,0:T(8,128)(2,1)S(1)}, bf16[528,256]{1,0:T(8,128)(2,1)S(1)}, u32[]{:S(2)}, u32[]{:S(2)}) %collective-permute-start) | collective-permute-done | bytes 270368 | tf_op jit(solution)/shard_map/ppermute | solution.py:248
  14.1 0.6 shard_map.32
  14.7 4.8 %collective-permute-start.1 = (bf16[528,256]{1,0:T(8,128)(2,1)S(1)}, bf16[528,256]{1,0:T(8,128)(2,1)S(1)}, u32[]{:S(2)}, u32[]{:S(2)}) collective-permute-start(bf16[528,256]{1,0:T(8,128)(2,1)S(1)} %get-tuple-element.15.a_ref), channel_id=1, source_target_pairs={{1,2},{2,1},{0,3},{3,0},{5,6},{6,5},{4,7},{7,4},{9,10},{10,9},{8,1... | collective-permute-start | bytes 811016 | tf_op jit(solution)/shard_map/ppermute | solution.py:252
  19.5 0.0 collective-permute-done.2.b_ref
  19.5 0.6 shard_map.34
  20.1 4.0 %collective-permute-start.3 = (bf16[528,256]{1,0:T(8,128)(2,1)S(1)}, bf16[528,256]{1,0:T(8,128)(2,1)S(1)}, u32[]{:S(2)}, u32[]{:S(2)}) collective-permute-start(bf16[528,256]{1,0:T(8,128)(2,1)S(1)} %get-tuple-element.19.a_ref), channel_id=1, source_target_pairs={{1,2},{2,1},{0,3},{3,0},{5,6},{6,5},{4,7},{7,4},{9,10},{10,9},{8,1... | collective-permute-start | bytes 811016 | tf_op jit(solution)/shard_map/ppermute | solution.py:254
  24.2 3.6 %collective-permute-done.1.b_ref = bf16[528,256]{1,0:T(8,128)(2,1)S(1)} collective-permute-done((bf16[528,256]{1,0:T(8,128)(2,1)S(1)}, bf16[528,256]{1,0:T(8,128)(2,1)S(1)}, u32[]{:S(2)}, u32[]{:S(2)}) %collective-permute-start.1) | collective-permute-done | bytes 270368 | tf_op jit(solution)/shard_map/ppermute | solution.py:252
  27.7 0.1 shard_map.33
  27.8 12.2 %collective-permute-start.4 = (bf16[528,256]{1,0:T(8,128)(2,1)S(1)}, bf16[528,256]{1,0:T(8,128)(2,1)S(1)}, u32[]{:S(2)}, u32[]{:S(2)}) collective-permute-start(bf16[528,256]{1,0:T(8,128)(2,1)S(1)} %get-tuple-element.16.k0_ref), channel_id=1, source_target_pairs={{0,1},{1,0},{2,3},{3,2},{4,5},{5,4},{6,7},{7,6},{8,9},{9,8},{10,11... | collective-permute-start | bytes 811016 | tf_op jit(solution)/shard_map/ppermute | solution.py:256
  40.0 0.0 collective-permute-done.3.b_ref
  40.0 0.6 shard_map.35
  40.6 3.4 %collective-permute-start.5 = (bf16[528,256]{1,0:T(8,128)(2,1)S(1)}, bf16[528,256]{1,0:T(8,128)(2,1)S(1)}, u32[]{:S(2)}, u32[]{:S(2)}) collective-permute-start(bf16[528,256]{1,0:T(8,128)(2,1)S(1)} %get-tuple-element.20.k1_ref), channel_id=1, source_target_pairs={{0,1},{1,0},{2,3},{3,2},{4,5},{5,4},{6,7},{7,6},{8,9},{9,8},{10,11... | collective-permute-start | bytes 811016 | tf_op jit(solution)/shard_map/ppermute | solution.py:258
  44.1 1.9 %collective-permute-start.6 = (f32[8,128]{1,0:T(8,128)S(1)}, f32[8,128]{1,0:T(8,128)S(1)}, u32[]{:S(2)}, u32[]{:S(2)}) collective-permute-start(f32[8,128]{1,0:T(8,128)S(1)} %get-tuple-element.21), channel_id=1, source_target_pairs={{0,4},{4,0},{8,12},{12,8},{16,20},{20,16},{24,28},{28,24},{32,36},... | collective-permute-start | bytes 12296 | tf_op jit(solution)/shard_map/ppermute | solution.py:239
  46.0 1.1 collective-permute-done.6
  47.1 3.4 %collective-permute-start.7 = (f32[8,128]{1,0:T(8,128)S(1)}, f32[8,128]{1,0:T(8,128)S(1)}, u32[]{:S(2)}, u32[]{:S(2)}) collective-permute-start(f32[8,128]{1,0:T(8,128)S(1)} %add.24), channel_id=1, source_target_pairs={{0,8},{4,12},{8,16},{12,20},{16,24},{20,28},{24,0},{28,4},{32,40},... | collective-permute-start | bytes 12296 | tf_op jit(solution)/shard_map/ppermute | solution.py:239
  50.5 3.3 %collective-permute-done.7 = f32[8,128]{1,0:T(8,128)S(1)} collective-permute-done((f32[8,128]{1,0:T(8,128)S(1)}, f32[8,128]{1,0:T(8,128)S(1)}, u32[]{:S(2)}, u32[]{:S(2)}) %collective-permute-start.7) | collective-permute-done | bytes 4128 | tf_op jit(solution)/shard_map/ppermute | solution.py:239
  53.8 3.7 %collective-permute-start.8 = (f32[8,128]{1,0:T(8,128)S(1)}, f32[8,128]{1,0:T(8,128)S(1)}, u32[]{:S(2)}, u32[]{:S(2)}) collective-permute-start(f32[8,128]{1,0:T(8,128)S(1)} %add.25), channel_id=1, source_target_pairs={{0,16},{4,20},{8,24},{12,28},{16,0},{20,4},{24,8},{28,12},{32,48},... | collective-permute-start | bytes 12296 | tf_op jit(solution)/shard_map/ppermute | solution.py:239
  57.5 3.3 %collective-permute-done.8 = f32[8,128]{1,0:T(8,128)S(1)} collective-permute-done((f32[8,128]{1,0:T(8,128)S(1)}, f32[8,128]{1,0:T(8,128)S(1)}, u32[]{:S(2)}, u32[]{:S(2)}) %collective-permute-start.8) | collective-permute-done | bytes 4128 | tf_op jit(solution)/shard_map/ppermute | solution.py:239
  60.8 14.5 %collective-permute-start.10 = (f32[8,128]{1,0:T(8,128)S(1)}, f32[8,128]{1,0:T(8,128)S(1)}, u32[]{:S(2)}, u32[]{:S(2)}) collective-permute-start(f32[8,128]{1,0:T(8,128)S(1)} %add.26), channel_id=1, source_target_pairs={{0,512},{4,516},{8,520},{12,524},{16,528},{20,532},{24,536},{28,54... | collective-permute-start | bytes 12296 | tf_op jit(solution)/shard_map/ppermute | solution.py:239
  75.4 1.9 %collective-permute-start.9 = (f32[8,128]{1,0:T(8,128)S(1)}, f32[8,128]{1,0:T(8,128)S(1)}, u32[]{:S(2)}, u32[]{:S(2)}) collective-permute-start(f32[8,128]{1,0:T(8,128)S(1)} %add.26), channel_id=1, source_target_pairs={{0,256},{4,260},{8,264},{12,268},{16,272},{20,276},{24,280},{28,28... | collective-permute-start | bytes 12296 | tf_op jit(solution)/shard_map/ppermute | solution.py:239
  77.3 0.0 collective-permute-done.10
  77.3 7.5 %collective-permute-done.9 = f32[8,128]{1,0:T(8,128)S(1)} collective-permute-done((f32[8,128]{1,0:T(8,128)S(1)}, f32[8,128]{1,0:T(8,128)S(1)}, u32[]{:S(2)}, u32[]{:S(2)}) %collective-permute-start.9) | collective-permute-done | bytes 4128 | tf_op jit(solution)/shard_map/ppermute | solution.py:239
  84.8 4.4 %collective-permute-start.11 = (f32[8,128]{1,0:T(8,128)S(1)}, f32[8,128]{1,0:T(8,128)S(1)}, u32[]{:S(2)}, u32[]{:S(2)}) collective-permute-start(f32[8,128]{1,0:T(8,128)S(1)} %add_add_fusion), channel_id=1, source_target_pairs={{0,128},{4,132},{8,136},{12,140},{16,144},{20,148},{24,152},{28,15... | collective-permute-start | bytes 12296 | tf_op jit(solution)/shard_map/ppermute | solution.py:239
  89.1 3.3 %collective-permute-done.11 = f32[8,128]{1,0:T(8,128)S(1)} collective-permute-done((f32[8,128]{1,0:T(8,128)S(1)}, f32[8,128]{1,0:T(8,128)S(1)}, u32[]{:S(2)}, u32[]{:S(2)}) %collective-permute-start.11) | collective-permute-done | bytes 4128 | tf_op jit(solution)/shard_map/ppermute | solution.py:239
  92.4 3.4 %collective-permute-start.12 = (f32[8,128]{1,0:T(8,128)S(1)}, f32[8,128]{1,0:T(8,128)S(1)}, u32[]{:S(2)}, u32[]{:S(2)}) collective-permute-start(f32[8,128]{1,0:T(8,128)S(1)} %add.29), channel_id=1, source_target_pairs={{0,64},{4,68},{8,72},{12,76},{16,80},{20,84},{24,88},{28,92},{32,9... | collective-permute-start | bytes 12296 | tf_op jit(solution)/shard_map/ppermute | solution.py:239
  95.8 3.3 %collective-permute-done.12 = f32[8,128]{1,0:T(8,128)S(1)} collective-permute-done((f32[8,128]{1,0:T(8,128)S(1)}, f32[8,128]{1,0:T(8,128)S(1)}, u32[]{:S(2)}, u32[]{:S(2)}) %collective-permute-start.12) | collective-permute-done | bytes 4128 | tf_op jit(solution)/shard_map/ppermute | solution.py:239
  99.1 3.8 %collective-permute-start.13 = (f32[8,128]{1,0:T(8,128)S(1)}, f32[8,128]{1,0:T(8,128)S(1)}, u32[]{:S(2)}, u32[]{:S(2)}) collective-permute-start(f32[8,128]{1,0:T(8,128)S(1)} %add.30), channel_id=1, source_target_pairs={{0,32},{4,36},{8,40},{12,44},{16,48},{20,52},{24,56},{28,60},{32,0... | collective-permute-start | bytes 12296 | tf_op jit(solution)/shard_map/ppermute | solution.py:239
  102.9 5.6 %collective-permute-done.13 = f32[8,128]{1,0:T(8,128)S(1)} collective-permute-done((f32[8,128]{1,0:T(8,128)S(1)}, f32[8,128]{1,0:T(8,128)S(1)}, u32[]{:S(2)}, u32[]{:S(2)}) %collective-permute-start.13) | collective-permute-done | bytes 4128 | tf_op jit(solution)/shard_map/ppermute | solution.py:239
  108.5 0.5 slice.3
  109.7 0.0 collective-permute-done.4.r0_ref
  109.7 0.0 collective-permute-done.5.r1_ref
  109.8 0.0 copy-done.1
  109.8 6.9 %shard_map.36 = bf16[1,896,1024]{2,1,0:T(8,128)(2,1)} custom-call(s32[1]{0:T(128)} %bitcast.own_ref, bf16[528,256]{1,0:T(8,128)(2,1)S(1)} %get-tuple-element.16.k0_ref, bf16[528,256]{1,0:T(8,128)(2,1)S(1)} %get-tuple-element.20.k1_ref, bf16[528,256]{1,0:T(8,128)(2,1)S(1)} %collective-permute-done.4.r0_ref, ...), custom_call_target="tpu_custom_call" | custom-call | flops 3758096384 | bytes 3670016 | tf_op jit(solution)/shard_map/pallas_call | solution.py:196
  (7 shorter events, 0.0 us)
Async XLA Ops:
  0.6 1.5 %copy-start = (bf16[1,896,1024]{2,1,0:T(8,128)(2,1)S(1)}, bf16[1,896,1024]{2,1,0:T(8,128)(2,1)}, u32[]{:S(2)}) copy-start(bf16[1,896,1024]{2,1,0:T(8,128)(2,1)} %x_ref.5) | copy-start | bytes 5505028
  2.8 11.2 %collective-permute-start = (bf16[528,256]{1,0:T(8,128)(2,1)S(1)}, bf16[528,256]{1,0:T(8,128)(2,1)S(1)}, u32[]{:S(2)}, u32[]{:S(2)}) collective-permute-start(bf16[528,256]{1,0:T(8,128)(2,1)S(1)} %get-tuple-element.14), channel_id=1, source_target_pairs={{0,1},{1,0},{2,3},{3,2},{4,5},{5,4},{6,7},{7,6},{8,9},{9,8},{10,11... | collective-permute-start | bytes 811016 | tf_op jit(solution)/shard_map/ppermute | solution.py:248
  7.5 102.2 %copy-start.1 = (bf16[1,896,1024]{2,1,0:T(8,128)(2,1)S(1)}, bf16[1,896,1024]{2,1,0:T(8,128)(2,1)}, u32[]{:S(2)}) copy-start(bf16[1,896,1024]{2,1,0:T(8,128)(2,1)} %x_ref.5) | copy-start | bytes 5505028
  7.5 12.0 %collective-permute-start.2 = (bf16[528,256]{1,0:T(8,128)(2,1)S(1)}, bf16[528,256]{1,0:T(8,128)(2,1)S(1)}, u32[]{:S(2)}, u32[]{:S(2)}) collective-permute-start(bf16[528,256]{1,0:T(8,128)(2,1)S(1)} %get-tuple-element.18), channel_id=1, source_target_pairs={{0,1},{1,0},{2,3},{3,2},{4,5},{5,4},{6,7},{7,6},{8,9},{9,8},{10,11... | collective-permute-start | bytes 811016 | tf_op jit(solution)/shard_map/ppermute | solution.py:250
  14.7 13.0 %collective-permute-start.1 = (bf16[528,256]{1,0:T(8,128)(2,1)S(1)}, bf16[528,256]{1,0:T(8,128)(2,1)S(1)}, u32[]{:S(2)}, u32[]{:S(2)}) collective-permute-start(bf16[528,256]{1,0:T(8,128)(2,1)S(1)} %get-tuple-element.15.a_ref), channel_id=1, source_target_pairs={{1,2},{2,1},{0,3},{3,0},{5,6},{6,5},{4,7},{7,4},{9,10},{10,9},{8,1... | collective-permute-start | bytes 811016 | tf_op jit(solution)/shard_map/ppermute | solution.py:252
  20.1 19.8 %collective-permute-start.3 = (bf16[528,256]{1,0:T(8,128)(2,1)S(1)}, bf16[528,256]{1,0:T(8,128)(2,1)S(1)}, u32[]{:S(2)}, u32[]{:S(2)}) collective-permute-start(bf16[528,256]{1,0:T(8,128)(2,1)S(1)} %get-tuple-element.19.a_ref), channel_id=1, source_target_pairs={{1,2},{2,1},{0,3},{3,0},{5,6},{6,5},{4,7},{7,4},{9,10},{10,9},{8,1... | collective-permute-start | bytes 811016 | tf_op jit(solution)/shard_map/ppermute | solution.py:254
  27.8 81.9 %collective-permute-start.4 = (bf16[528,256]{1,0:T(8,128)(2,1)S(1)}, bf16[528,256]{1,0:T(8,128)(2,1)S(1)}, u32[]{:S(2)}, u32[]{:S(2)}) collective-permute-start(bf16[528,256]{1,0:T(8,128)(2,1)S(1)} %get-tuple-element.16.k0_ref), channel_id=1, source_target_pairs={{0,1},{1,0},{2,3},{3,2},{4,5},{5,4},{6,7},{7,6},{8,9},{9,8},{10,11... | collective-permute-start | bytes 811016 | tf_op jit(solution)/shard_map/ppermute | solution.py:256
  40.6 69.1 %collective-permute-start.5 = (bf16[528,256]{1,0:T(8,128)(2,1)S(1)}, bf16[528,256]{1,0:T(8,128)(2,1)S(1)}, u32[]{:S(2)}, u32[]{:S(2)}) collective-permute-start(bf16[528,256]{1,0:T(8,128)(2,1)S(1)} %get-tuple-element.20.k1_ref), channel_id=1, source_target_pairs={{0,1},{1,0},{2,3},{3,2},{4,5},{5,4},{6,7},{7,6},{8,9},{9,8},{10,11... | collective-permute-start | bytes 811016 | tf_op jit(solution)/shard_map/ppermute | solution.py:258
  44.1 3.1 %collective-permute-start.6 = (f32[8,128]{1,0:T(8,128)S(1)}, f32[8,128]{1,0:T(8,128)S(1)}, u32[]{:S(2)}, u32[]{:S(2)}) collective-permute-start(f32[8,128]{1,0:T(8,128)S(1)} %get-tuple-element.21), channel_id=1, source_target_pairs={{0,4},{4,0},{8,12},{12,8},{16,20},{20,16},{24,28},{28,24},{32,36},... | collective-permute-start | bytes 12296 | tf_op jit(solution)/shard_map/ppermute | solution.py:239
  47.1 6.7 %collective-permute-start.7 = (f32[8,128]{1,0:T(8,128)S(1)}, f32[8,128]{1,0:T(8,128)S(1)}, u32[]{:S(2)}, u32[]{:S(2)}) collective-permute-start(f32[8,128]{1,0:T(8,128)S(1)} %add.24), channel_id=1, source_target_pairs={{0,8},{4,12},{8,16},{12,20},{16,24},{20,28},{24,0},{28,4},{32,40},... | collective-permute-start | bytes 12296 | tf_op jit(solution)/shard_map/ppermute | solution.py:239
  53.8 7.0 %collective-permute-start.8 = (f32[8,128]{1,0:T(8,128)S(1)}, f32[8,128]{1,0:T(8,128)S(1)}, u32[]{:S(2)}, u32[]{:S(2)}) collective-permute-start(f32[8,128]{1,0:T(8,128)S(1)} %add.25), channel_id=1, source_target_pairs={{0,16},{4,20},{8,24},{12,28},{16,0},{20,4},{24,8},{28,12},{32,48},... | collective-permute-start | bytes 12296 | tf_op jit(solution)/shard_map/ppermute | solution.py:239
  60.8 16.5 %collective-permute-start.10 = (f32[8,128]{1,0:T(8,128)S(1)}, f32[8,128]{1,0:T(8,128)S(1)}, u32[]{:S(2)}, u32[]{:S(2)}) collective-permute-start(f32[8,128]{1,0:T(8,128)S(1)} %add.26), channel_id=1, source_target_pairs={{0,512},{4,516},{8,520},{12,524},{16,528},{20,532},{24,536},{28,54... | collective-permute-start | bytes 12296 | tf_op jit(solution)/shard_map/ppermute | solution.py:239
  75.4 9.4 %collective-permute-start.9 = (f32[8,128]{1,0:T(8,128)S(1)}, f32[8,128]{1,0:T(8,128)S(1)}, u32[]{:S(2)}, u32[]{:S(2)}) collective-permute-start(f32[8,128]{1,0:T(8,128)S(1)} %add.26), channel_id=1, source_target_pairs={{0,256},{4,260},{8,264},{12,268},{16,272},{20,276},{24,280},{28,28... | collective-permute-start | bytes 12296 | tf_op jit(solution)/shard_map/ppermute | solution.py:239
  84.8 7.6 %collective-permute-start.11 = (f32[8,128]{1,0:T(8,128)S(1)}, f32[8,128]{1,0:T(8,128)S(1)}, u32[]{:S(2)}, u32[]{:S(2)}) collective-permute-start(f32[8,128]{1,0:T(8,128)S(1)} %add_add_fusion), channel_id=1, source_target_pairs={{0,128},{4,132},{8,136},{12,140},{16,144},{20,148},{24,152},{28,15... | collective-permute-start | bytes 12296 | tf_op jit(solution)/shard_map/ppermute | solution.py:239
  92.4 6.7 %collective-permute-start.12 = (f32[8,128]{1,0:T(8,128)S(1)}, f32[8,128]{1,0:T(8,128)S(1)}, u32[]{:S(2)}, u32[]{:S(2)}) collective-permute-start(f32[8,128]{1,0:T(8,128)S(1)} %add.29), channel_id=1, source_target_pairs={{0,64},{4,68},{8,72},{12,76},{16,80},{20,84},{24,88},{28,92},{32,9... | collective-permute-start | bytes 12296 | tf_op jit(solution)/shard_map/ppermute | solution.py:239
  99.1 9.4 %collective-permute-start.13 = (f32[8,128]{1,0:T(8,128)S(1)}, f32[8,128]{1,0:T(8,128)S(1)}, u32[]{:S(2)}, u32[]{:S(2)}) collective-permute-start(f32[8,128]{1,0:T(8,128)S(1)} %add.30), channel_id=1, source_target_pairs={{0,32},{4,36},{8,40},{12,44},{16,48},{20,52},{24,56},{28,60},{32,0... | collective-permute-start | bytes 12296 | tf_op jit(solution)/shard_map/ppermute | solution.py:239

commit v2 on v1

v2 whole, which is shorter than its diff:
```python
import math

import jax
import jax.numpy as jnp
from jax import lax
from jax.experimental import pallas as pl
from jax.experimental.pallas import tpu as pltpu
from jax.sharding import Mesh
from jax.sharding import PartitionSpec as P

R = 3584
C = 1024
B = 256
H = 128
ROWS = 2 * B + 16

FULL = ((1, 0), (2, 1), (3, 2), (3, 0))
HALF = ((2, 0, 0), (2, 0, 1), (3, 1, 0), (3, 1, 1))


def pick(p, values):
    out = jnp.int32(values[0])
    for k in range(1, len(values)):
        out = jnp.where(p == k, jnp.int32(values[k]), out)
    return out


def lower(shape=(H, H)):
    rows = lax.broadcasted_iota(jnp.int32, shape, 0)
    cols = lax.broadcasted_iota(jnp.int32, shape, 1)
    return rows, cols


def columns(x_ref, start, width):
    return x_ref[0, :, pl.ds(pl.multiple_of(start, H), width)]


def outer(a, b):
    return lax.dot_general(a, b, (((0,), (0,)), ((), ())), preferred_element_type=jnp.float32)


def quarter(x_ref, p, out_ref, slot):
    own = columns(x_ref, p * B, B)
    diag = outer(own, own)
    fi, fj = (pick(p, [f[k] for f in FULL]) for k in (0, 1))
    out_ref[slot, 0:B, :] = outer(columns(x_ref, fi * B, B), columns(x_ref, fj * B, B)).astype(jnp.bfloat16)
    hi, hj, part = (pick(p, [h[k] for h in HALF]) for k in (0, 1, 2))
    out_ref[slot, B : B + H, :] = outer(
        columns(x_ref, hi * B + part * H, H), columns(x_ref, hj * B, B)
    ).astype(jnp.bfloat16)
    rows, cols = lower()
    first, last = diag[:H, :H], diag[H:, H:]
    out_ref[slot, B + H : 2 * B, :H] = diag[H:, :H].astype(jnp.bfloat16)
    out_ref[slot, B + H : 2 * B, H:] = jnp.where(rows > cols, first, last).astype(jnp.bfloat16)
    line = jnp.sum(jnp.where(rows == cols, first, 0.0), axis=0, keepdims=True)
    line = jnp.broadcast_to(jnp.concatenate([line, line], axis=1), (16, B))
    out_ref[slot, 2 * B :, :] = line.astype(jnp.bfloat16)


def first_kernel(own_ref, x_ref, out_ref, sum_ref):
    wide = x_ref[0].astype(jnp.float32)
    squares = jnp.sum(wide * wide, axis=0, keepdims=True)
    total = jnp.sum(squares, axis=1, keepdims=True)
    sum_ref[...] = jnp.broadcast_to(total, (8, H))
    for slot in range(2):
        quarter(x_ref, 2 * (1 - own_ref[0]) + slot, out_ref, slot)


def second_kernel(own_ref, x_ref, keep_ref):
    for slot in range(2):
        quarter(x_ref, 2 * own_ref[0] + slot, keep_ref, slot)


def add_kernel(a_ref, b_ref, out_ref):
    out_ref[...] = (a_ref[...].astype(jnp.float32) + b_ref[...].astype(jnp.float32)).astype(jnp.bfloat16)


def final_kernel(own_ref, keep_ref, recv_ref, x_ref, out_ref, gram, poly, scale):
    @pl.when(pl.program_id(0) == 0)
    def _():
        mine = own_ref[0] == 0
        rows, cols = lower()
        squares = jnp.zeros((H, B), jnp.float32)
        for p in range(4):
            slot, low = p % 2, p < 2

            def get(part):
                k, r = keep_ref[slot, part, :], recv_ref[slot, part, :]
                return jnp.where(mine, k, r) if low else jnp.where(mine, r, k)

            def put(i, j, block):
                gram[i : i + block.shape[0], j : j + block.shape[1]] = block
                gram[j : j + block.shape[1], i : i + block.shape[0]] = block.T

            block = get(slice(0, B))
            fi, fj = FULL[p]
            put(fi * B, fj * B, block)
            wide = block.astype(jnp.float32)
            squares += 2.0 * (wide[:H] * wide[:H] + wide[H:] * wide[H:])
            block = get(slice(B, B + H))
            hi, hj, part = HALF[p]
            put(hi * B + part * H, hj * B, block)
            wide = block.astype(jnp.float32)
            squares += 2.0 * wide * wide
            block = get(slice(B + H, 2 * B))
            put(p * B + H, p * B, block[:, :H])
            fold = block[:, H:].astype(jnp.float32)
            flip = fold.T
            line = get(slice(2 * B, 2 * B + 16))[0:1, :H].astype(jnp.float32)
            upper = jnp.where(rows < cols, flip, jnp.where(rows == cols, jnp.broadcast_to(line, (H, H)), fold))
            second = jnp.where(rows > cols, flip, fold)
            gram[p * B : p * B + H, p * B : p * B + H] = upper.astype(jnp.bfloat16)
            gram[p * B + H : (p + 1) * B, p * B + H : (p + 1) * B] = second.astype(jnp.bfloat16)
            wide = block[:, :H].astype(jnp.float32)
            squares += jnp.concatenate([2.0 * wide * wide, upper * upper + second * second], axis=1)
        norm = jnp.sqrt(jnp.sum(jnp.sum(squares, axis=0, keepdims=True), axis=1, keepdims=True))
        factor = 1.0 / (norm + 1e-07)
        scale[...] = jnp.broadcast_to(math.sqrt(R) * jnp.sqrt(factor), (8, H))
        for i in range(4):
            for j in range(i + 1):
                product = jnp.dot(
                    gram[i * B : (i + 1) * B, :], gram[:, j * B : (j + 1) * B], preferred_element_type=jnp.float32
                )
                block = gram[i * B : (i + 1) * B, j * B : (j + 1) * B].astype(jnp.float32)
                block = (-4.775 * factor * block + 2.0315 * factor * factor * product).astype(jnp.bfloat16)
                poly[i * B : (i + 1) * B, j * B : (j + 1) * B] = block
                if i != j:
                    poly[j * B : (j + 1) * B, i * B : (i + 1) * B] = block.T

    x = x_ref[0]
    applied = jnp.dot(x, poly[...], preferred_element_type=jnp.float32)
    out_ref[0] = (scale[0:1, 0:1] * (3.4445 * x.astype(jnp.float32) + applied)).astype(jnp.bfloat16)


HALVES = jax.ShapeDtypeStruct((2, ROWS, B), jnp.bfloat16)
TILE = jax.ShapeDtypeStruct((8, H), jnp.float32)
SMEM = pl.BlockSpec(memory_space=pltpu.SMEM)
VMEM = pl.BlockSpec(memory_space=pltpu.VMEM)


def call(kernel, in_specs, outs, flops, nbytes, limit):
    return pl.pallas_call(
        kernel,
        out_shape=outs,
        in_specs=in_specs,
        out_specs=[VMEM] * len(outs),
        cost_estimate=pl.CostEstimate(flops=flops, bytes_accessed=nbytes, transcendentals=0),
        compiler_params=pltpu.CompilerParams(vmem_limit_bytes=limit << 20),
    )


def add_halves(a, b):
    return call(add_kernel, [VMEM] * 2, [HALVES], 2 * ROWS * B, 12 * ROWS * B, 8)(a, b)[0]


def finish(own, keep, recv, x, rows):
    step = 128
    return pl.pallas_call(
        final_kernel,
        grid=(rows // step,),
        out_shape=jax.ShapeDtypeStruct((1, rows, C), jnp.bfloat16),
        in_specs=[SMEM] + [VMEM] * 2 + [pl.BlockSpec((1, step, C), lambda i: (0, i, 0))],
        out_specs=pl.BlockSpec((1, step, C), lambda i: (0, i, 0)),
        scratch_shapes=[
            pltpu.VMEM((C, C), jnp.bfloat16),
            pltpu.VMEM((C, C), jnp.bfloat16),
            pltpu.VMEM((8, H), jnp.float32),
        ],
        cost_estimate=pl.CostEstimate(flops=4 * rows * C * C, bytes_accessed=4 * rows * C, transcendentals=0),
        compiler_params=pltpu.CompilerParams(vmem_limit_bytes=24 << 20),
    )(own, keep, recv, x)


PAIR = [(0, 1), (1, 0), (2, 3), (3, 2)]
CROSS = [(1, 2), (2, 1), (0, 3), (3, 0)]
DP = ("z", "y_hi", "x", "core")
Z, Y_HI, X, CORES = 12, 2, 4, 2


def over(line, axes):
    count = lax.axis_size(axes)
    parts = lax.all_to_all(jnp.broadcast_to(line, (count, H)), axes, 0, 0, tiled=True)
    return jnp.sum(parts, axis=0, keepdims=True)


def shards(gradient):
    rows = gradient.shape[1]
    place = lax.axis_index("slab")
    own = jnp.where((place == 1) | (place == 2), 1, 0).astype(jnp.int32).reshape(1)
    work = rows * B * B * 10
    send, tile = call(first_kernel, [SMEM, VMEM], [HALVES, TILE], work, 2 * rows * C, 16)(own, gradient)
    got = lax.ppermute(send, "slab", PAIR)
    (keep,) = call(second_kernel, [SMEM, VMEM], [HALVES], work, 2 * rows * C, 16)(own, gradient)
    total = over(tile[0:1], ("x", "core"))
    got, total = lax.optimization_barrier((got, total))
    half = add_halves(keep, got)
    crossed = lax.ppermute(half, "slab", CROSS)
    half, total = lax.optimization_barrier((half, total))
    total = over(total, ("z",))
    crossed, total = lax.optimization_barrier((crossed, total))
    whole = add_halves(half, crossed)
    other = lax.ppermute(whole, "slab", PAIR)
    whole, total = lax.optimization_barrier((whole, total))
    total = over(total, ("y_hi", "slab"))
    other, total = lax.optimization_barrier((other, total))
    update = finish(own, whole, other, gradient, rows)
    entries = gradient.size * lax.axis_size(DP) * lax.axis_size("slab")
    return update, jnp.sqrt(total[0, 0] / entries)


def solution(mesh):
    named = Mesh(mesh.devices.reshape(Z, Y_HI, X, CORES, mesh.shape["slab"]), DP + ("slab",))
    placed = P(DP, "slab", None)
    return jax.shard_map(shards, mesh=named, in_specs=(placed,), out_specs=(placed, P()), check_vma=False)
```

time: 118 us -> 75.9 us (0.64)
  starting transfers between devices: 67.4 us -> 14.3 us
  blocking collectives: 0 us -> 40.8 us
  waiting for transfers between devices: 34.7 us -> 6.78 us
  Pallas kernels: 10.9 us -> 9 us
    ppermute x14 -> x3, starting transfers between devices: 67.4 us -> 9.99 us  [the longest x1 4.83 us: shards(): crossed = lax.ppermute(half, 'slab', CROSS)]
    all_to_all x0 -> x2, blocking collectives: none -> 40.8 us  [over(): lax.all_to_all(jnp.broadcast_to(line, (count, H)), axes, 0, 0, tiled=True)]
    ppermute x14 -> x3, waiting for transfers between devices: 34.7 us -> 2.52 us  [the longest x1 2.51 us: shards(): got = lax.ppermute(send, 'slab', PAIR)]
    all_to_all x0 -> x1, starting transfers between devices: none -> 4.3 us  [over(): lax.all_to_all(jnp.broadcast_to(line, (count, H)), axes, 0, 0, tiled=True)]
    all_to_all x0 -> x1, waiting for transfers between devices: none -> 4.26 us  [over(): lax.all_to_all(jnp.broadcast_to(line, (count, H)), axes, 0, 0, tiled=True)]
    pallas_call x6 -> x4, Pallas kernels: 4.04 us -> 2.17 us  [the longest x1 0.97 us: shards(): call(first_kernel, [SMEM, VMEM], [HALVES, TILE], work, 2 * rows * C, 16)]
  transfers between devices with their start and end apart: 14 -> 4, of which waited for: 9 -> 2; matrix products, arithmetic and copies ran while one was open for 0% -> 1% of each run, Pallas kernels for 3% -> 1%
where the time goes in v2:
time: 75.9 us; the launch traced here: 74.9 us
  blocking collectives  40.8 us (54%)
  starting transfers between devices  14.3 us (19%)
  Pallas kernels  9 us (12%)
  waiting for transfers between devices  6.78 us (9%)
  local copies, waits for them, and re-layouts  2.1 us (3%)
  between operations  1.94 us (3%)
    all_to_all x2, blocking collectives, over(): lax.all_to_all(jnp.broadcast_to(line, (count, H)), axes, 0, 0, tiled=True)  40.8 us
    pallas_call x1, Pallas kernels, finish(): pl.pallas_call(final_kernel, grid=(rows // step,), out_shape=jax.ShapeDty...  6.82 us
    ppermute x1, starting transfers between devices, shards(): crossed = lax.ppermute(half, 'slab', CROSS)  4.83 us
    all_to_all x1, starting transfers between devices, over(): lax.all_to_all(jnp.broadcast_to(line, (count, H)), axes, 0, 0, tiled=True)  4.3 us
    all_to_all x1, waiting for transfers between devices, over(): lax.all_to_all(jnp.broadcast_to(line, (count, H)), axes, 0, 0, tiled=True)  4.26 us
    ppermute x1, starting transfers between devices, shards(): got = lax.ppermute(send, 'slab', PAIR)  3.24 us
    ppermute x1, waiting for transfers between devices, shards(): got = lax.ppermute(send, 'slab', PAIR)  2.51 us
    ppermute x1, starting transfers between devices, shards(): other = lax.ppermute(whole, 'slab', PAIR)  1.92 us
  transfers between devices with their start and end apart: 4, of which 2 were waited for; matrix products, arithmetic and copies ran while one was open for 1% of the time, Pallas kernels for 1%

profile of v2, /device:TPU:56, one launch (start us, length us, event | category | flops | bytes accessed | tf_op | source)
XLA Modules:
  0.0 74.9 jit_solution(14716186307604561299)
XLA Ops:
  0.6 0.0 copy-start
  0.6 1.5 %copy-done = bf16[1,896,1024]{2,1,0:T(8,128)(2,1)S(1)} copy-done((bf16[1,896,1024]{2,1,0:T(8,128)(2,1)S(1)}, bf16[1,896,1024]{2,1,0:T(8,128)(2,1)}, u32[]{:S(2)}) %copy-start) | copy-done | bytes 1835032
  2.1 0.0 copy-start.1
  2.1 1.0 %shard_map.31 = (bf16[2,528,256]{2,1,0:T(8,128)(2,1)S(1)}, f32[8,128]{1,0:T(8,128)S(1)}) custom-call(s32[1]{0:T(128)} %bitcast.own_ref, bf16[1,896,1024]{2,1,0:T(8,128)(2,1)S(1)} %copy-done), custom_call_target="tpu_custom_call" | custom-call | flops 587202560 | bytes 1835008 | tf_op jit(solution)/shard_map/pallas_call | solution.py:191
  3.1 3.2 %collective-permute-start = (bf16[2,528,256]{2,1,0:T(8,128)(2,1)S(1)}, bf16[2,528,256]{2,1,0:T(8,128)(2,1)S(1)}, u32[]{:S(2)}, u32[]{:S(2)}) collective-permute-start(bf16[2,528,256]{2,1,0:T(8,128)(2,1)S(1)} %get-tuple-element.14), channel_id=1, source_target_pairs={{0,1},{1,0},{2,3},{3,2},{4,5},{5,4},{6,7},{7,6},{8,9},{9,8},{10,11... | collective-permute-start | bytes 1622024 | tf_op jit(solution)/shard_map/ppermute | solution.py:192
  6.4 0.6 broadcast_in_dim.24
  7.0 4.3 %all-to-all-start = ((f32[8,1,128]{2,1,0:T(1,128)}), f32[8,1,128]{2,1,0:T(1,128)S(1)}, u32[]{:S(2)}, u32[]{:S(2)}) async-start(f32[8,1,128]{2,1,0:T(1,128)} %broadcast_in_dim.24), calls=%async_computation | async-start | bytes 8192 | tf_op jit(solution)/shard_map/all_to_all | solution.py:182
  11.3 0.0 copy-done.1
  11.3 0.9 %shard_map.30.a_ref = bf16[2,528,256]{2,1,0:T(8,128)(2,1)S(1)} custom-call(s32[1]{0:T(128)} %bitcast.own_ref, bf16[1,896,1024]{2,1,0:T(8,128)(2,1)S(1)} %copy-done.1), custom_call_target="tpu_custom_call" | custom-call | flops 587202560 | bytes 1835008 | tf_op jit(solution)/shard_map/pallas_call | solution.py:193
  12.2 4.3 %all-to-all-done = f32[8,1,128]{2,1,0:T(1,128)S(1)} async-done(((f32[8,1,128]{2,1,0:T(1,128)}), f32[8,1,128]{2,1,0:T(1,128)S(1)}, u32[]{:S(2)}, u32[]{:S(2)}) %all-to-all-start) | async-done | bytes 4128 | tf_op jit(solution)/shard_map/all_to_all | solution.py:182
  16.5 2.5 %collective-permute-done.b_ref = bf16[2,528,256]{2,1,0:T(8,128)(2,1)S(1)} collective-permute-done((bf16[2,528,256]{2,1,0:T(8,128)(2,1)S(1)}, bf16[2,528,256]{2,1,0:T(8,128)(2,1)S(1)}, u32[]{:S(2)}, u32[]{:S(2)}) %collective-permute-start) | collective-permute-done | bytes 540704 | tf_op jit(solution)/shard_map/ppermute | solution.py:192
  19.0 0.1 shard_map.32.a_ref
  19.2 4.8 %collective-permute-start.1 = (bf16[2,528,256]{2,1,0:T(8,128)(2,1)S(1)}, bf16[2,528,256]{2,1,0:T(8,128)(2,1)S(1)}, u32[]{:S(2)}, u32[]{:S(2)}) collective-permute-start(bf16[2,528,256]{2,1,0:T(8,128)(2,1)S(1)} %shard_map.32.a_ref), channel_id=1, source_target_pairs={{1,2},{2,1},{0,3},{3,0},{5,6},{6,5},{4,7},{7,4},{9,10},{10,9},{8,1... | collective-permute-start | bytes 1622024 | tf_op jit(solution)/shard_map/ppermute | solution.py:197
  24.0 25.1 %all_to_all.18 = f32[12,1,128]{2,1,0:T(1,128)S(1)} all-to-all(f32[12,1,128]{2,1,0:T(1,128)S(1)} %broadcast_in_dim.26), channel_id=1, replica_groups=mesh['z'=12,'y_hi'=2,'x'=4,'core'=2,'slab'=4] {'z'}, dimensions={0} | all-to-all | bytes 12288 | tf_op jit(solution)/shard_map/all_to_all | solution.py:182
  49.1 0.0 collective-permute-done.1.b_ref
  49.1 0.1 shard_map.33.keep_ref
  49.2 1.9 %collective-permute-start.2 = (bf16[2,528,256]{2,1,0:T(8,128)(2,1)S(1)}, bf16[2,528,256]{2,1,0:T(8,128)(2,1)S(1)}, u32[]{:S(2)}, u32[]{:S(2)}) collective-permute-start(bf16[2,528,256]{2,1,0:T(8,128)(2,1)S(1)} %shard_map.33.keep_ref), channel_id=1, source_target_pairs={{0,1},{1,0},{2,3},{3,2},{4,5},{5,4},{6,7},{7,6},{8,9},{9,8},{10,11... | collective-permute-start | bytes 1622024 | tf_op jit(solution)/shard_map/ppermute | solution.py:202
  51.2 15.7 %all_to_all.19 = f32[8,1,128]{2,1,0:T(1,128)S(1)} all-to-all(f32[8,1,128]{2,1,0:T(1,128)S(1)} %broadcast_in_dim.28), channel_id=1, replica_groups=mesh['z'=12,'y_hi'=2,'x'=4,'core'=2,'slab'=4] {'y_hi','slab'}, dimensions={0} | all-to-all | bytes 8192 | tf_op jit(solution)/shard_map/all_to_all | solution.py:182
  66.9 0.0 collective-permute-done.2.recv_ref
  67.0 6.8 %shard_map.34 = bf16[1,896,1024]{2,1,0:T(8,128)(2,1)} custom-call(s32[1]{0:T(128)} %bitcast.own_ref, bf16[2,528,256]{2,1,0:T(8,128)(2,1)S(1)} %shard_map.33.keep_ref, bf16[2,528,256]{2,1,0:T(8,128)(2,1)S(1)} %collective-permute-done.2.recv_ref, bf16[1,896,1024]{2,1,0:T(8,128)(2,1)S(1)} %copy-done.1), custom_call_target="tpu_custom_call" | custom-call | flops 3758096384 | bytes 3670016 | tf_op jit(solution)/shard_map/pallas_call | solution.py:158
  (6 shorter events, 0.1 us)
Async XLA Ops:
  0.6 1.5 %copy-start = (bf16[1,896,1024]{2,1,0:T(8,128)(2,1)S(1)}, bf16[1,896,1024]{2,1,0:T(8,128)(2,1)}, u32[]{:S(2)}) copy-start(bf16[1,896,1024]{2,1,0:T(8,128)(2,1)} %x_ref.5) | copy-start | bytes 5505028
  2.1 9.1 %copy-start.1 = (bf16[1,896,1024]{2,1,0:T(8,128)(2,1)S(1)}, bf16[1,896,1024]{2,1,0:T(8,128)(2,1)}, u32[]{:S(2)}) copy-start(bf16[1,896,1024]{2,1,0:T(8,128)(2,1)} %x_ref.5) | copy-start | bytes 5505028
  3.1 15.9 %collective-permute-start = (bf16[2,528,256]{2,1,0:T(8,128)(2,1)S(1)}, bf16[2,528,256]{2,1,0:T(8,128)(2,1)S(1)}, u32[]{:S(2)}, u32[]{:S(2)}) collective-permute-start(bf16[2,528,256]{2,1,0:T(8,128)(2,1)S(1)} %get-tuple-element.14), channel_id=1, source_target_pairs={{0,1},{1,0},{2,3},{3,2},{4,5},{5,4},{6,7},{7,6},{8,9},{9,8},{10,11... | collective-permute-start | bytes 1622024 | tf_op jit(solution)/shard_map/ppermute | solution.py:192
  7.0 9.5 %all-to-all-start = ((f32[8,1,128]{2,1,0:T(1,128)}), f32[8,1,128]{2,1,0:T(1,128)S(1)}, u32[]{:S(2)}, u32[]{:S(2)}) async-start(f32[8,1,128]{2,1,0:T(1,128)} %broadcast_in_dim.24), calls=%async_computation | async-start | bytes 8192 | tf_op jit(solution)/shard_map/all_to_all | solution.py:182
  19.2 29.9 %collective-permute-start.1 = (bf16[2,528,256]{2,1,0:T(8,128)(2,1)S(1)}, bf16[2,528,256]{2,1,0:T(8,128)(2,1)S(1)}, u32[]{:S(2)}, u32[]{:S(2)}) collective-permute-start(bf16[2,528,256]{2,1,0:T(8,128)(2,1)S(1)} %shard_map.32.a_ref), channel_id=1, source_target_pairs={{1,2},{2,1},{0,3},{3,0},{5,6},{6,5},{4,7},{7,4},{9,10},{10,9},{8,1... | collective-permute-start | bytes 1622024 | tf_op jit(solution)/shard_map/ppermute | solution.py:197
  49.2 17.7 %collective-permute-start.2 = (bf16[2,528,256]{2,1,0:T(8,128)(2,1)S(1)}, bf16[2,528,256]{2,1,0:T(8,128)(2,1)S(1)}, u32[]{:S(2)}, u32[]{:S(2)}) collective-permute-start(bf16[2,528,256]{2,1,0:T(8,128)(2,1)S(1)} %shard_map.33.keep_ref), channel_id=1, source_target_pairs={{0,1},{1,0},{2,3},{3,2},{4,5},{5,4},{6,7},{7,6},{8,9},{9,8},{10,11... | collective-permute-start | bytes 1622024 | tf_op jit(solution)/shard_map/ppermute | solution.py:202

commit v3 on v2

v3 whole, which is shorter than its diff:
```python
import math

import jax
import jax.numpy as jnp
from jax import lax
from jax.experimental import pallas as pl
from jax.experimental.pallas import tpu as pltpu
from jax.sharding import Mesh
from jax.sharding import PartitionSpec as P

R = 3584
C = 1024
B = 256
H = 128
REST = B + 16
LARGE = 2 * B + REST

FULL = ((1, 0), (2, 1), (3, 2), (3, 0))
HALF = ((2, 0, 0), (2, 0, 1), (3, 1, 0), (3, 1, 1))


def pick(p, values):
    out = jnp.int32(values[0])
    for k in range(1, len(values)):
        out = jnp.where(p == k, jnp.int32(values[k]), out)
    return out


def lower(shape=(H, H)):
    rows = lax.broadcasted_iota(jnp.int32, shape, 0)
    cols = lax.broadcasted_iota(jnp.int32, shape, 1)
    return rows, cols


def columns(x_ref, start, width):
    return x_ref[0, :, pl.ds(pl.multiple_of(start, H), width)]


def outer(a, b):
    return lax.dot_general(a, b, (((0,), (0,)), ((), ())), preferred_element_type=jnp.float32)


def whole_block(x_ref, p, out_ref, at):
    i, j = (pick(p, [f[k] for f in FULL]) for k in (0, 1))
    out_ref[at : at + B, :] = outer(columns(x_ref, i * B, B), columns(x_ref, j * B, B)).astype(jnp.bfloat16)


def rest(x_ref, p, out_ref, at):
    i, j, part = (pick(p, [h[k] for h in HALF]) for k in (0, 1, 2))
    out_ref[at : at + H, :] = outer(
        columns(x_ref, i * B + part * H, H), columns(x_ref, j * B, B)
    ).astype(jnp.bfloat16)
    own = columns(x_ref, p * B, B)
    diag = outer(own, own)
    rows, cols = lower()
    first, last = diag[:H, :H], diag[H:, H:]
    out_ref[at + H : at + B, :H] = diag[H:, :H].astype(jnp.bfloat16)
    out_ref[at + H : at + B, H:] = jnp.where(rows > cols, first, last).astype(jnp.bfloat16)
    line = jnp.sum(jnp.where(rows == cols, first, 0.0), axis=0, keepdims=True)
    line = jnp.broadcast_to(jnp.concatenate([line, line], axis=1), (16, B))
    out_ref[at + B : at + REST, :] = line.astype(jnp.bfloat16)


def large_part(x_ref, half, out_ref):
    whole_block(x_ref, 2 * half, out_ref, 0)
    rest(x_ref, 2 * half, out_ref, B)
    whole_block(x_ref, 2 * half + 1, out_ref, B + REST)


def first_kernel(own_ref, x_ref, out_ref, sum_ref):
    wide = x_ref[0].astype(jnp.float32)
    squares = jnp.sum(wide * wide, axis=0, keepdims=True)
    total = jnp.sum(squares, axis=1, keepdims=True)
    sum_ref[...] = jnp.broadcast_to(total, (8, H))
    large_part(x_ref, 1 - own_ref[0], out_ref)


def second_kernel(own_ref, x_ref, out_ref):
    rest(x_ref, 2 * (1 - own_ref[0]) + 1, out_ref, 0)


def third_kernel(own_ref, x_ref, keep_a_ref, keep_b_ref):
    large_part(x_ref, own_ref[0], keep_a_ref)
    rest(x_ref, 2 * own_ref[0] + 1, keep_b_ref, 0)


def add_kernel(a_ref, b_ref, out_ref):
    out_ref[...] = (a_ref[...].astype(jnp.float32) + b_ref[...].astype(jnp.float32)).astype(jnp.bfloat16)


def final_kernel(own_ref, keep_a_ref, keep_b_ref, recv_a_ref, recv_b_ref, x_ref, out_ref, gram, poly, scale):
    @pl.when(pl.program_id(0) == 0)
    def _():
        mine = own_ref[0] == 0
        rows, cols = lower()
        squares = jnp.zeros((H, B), jnp.float32)
        for p in range(4):
            low = p < 2

            def get(small, start, size):
                keep_ref, recv_ref = (keep_b_ref, recv_b_ref) if small else (keep_a_ref, recv_a_ref)
                k, r = keep_ref[start : start + size, :], recv_ref[start : start + size, :]
                return jnp.where(mine, k, r) if low else jnp.where(mine, r, k)

            small = p % 2 == 1
            top, base = (B + REST, 0) if small else (0, B)

            def put(i, j, block):
                gram[i : i + block.shape[0], j : j + block.shape[1]] = block
                gram[j : j + block.shape[1], i : i + block.shape[0]] = block.T

            block = get(False, top, B)
            fi, fj = FULL[p]
            put(fi * B, fj * B, block)
            wide = block.astype(jnp.float32)
            squares += 2.0 * (wide[:H] * wide[:H] + wide[H:] * wide[H:])
            block = get(small, base, H)
            hi, hj, part = HALF[p]
            put(hi * B + part * H, hj * B, block)
            wide = block.astype(jnp.float32)
            squares += 2.0 * wide * wide
            block = get(small, base + H, H)
            put(p * B + H, p * B, block[:, :H])
            fold = block[:, H:].astype(jnp.float32)
            flip = fold.T
            line = get(small, base + B, 16)[0:1, :H].astype(jnp.float32)
            upper = jnp.where(rows < cols, flip, jnp.where(rows == cols, jnp.broadcast_to(line, (H, H)), fold))
            second = jnp.where(rows > cols, flip, fold)
            gram[p * B : p * B + H, p * B : p * B + H] = upper.astype(jnp.bfloat16)
            gram[p * B + H : (p + 1) * B, p * B + H : (p + 1) * B] = second.astype(jnp.bfloat16)
            wide = block[:, :H].astype(jnp.float32)
            squares += jnp.concatenate([2.0 * wide * wide, upper * upper + second * second], axis=1)
        norm = jnp.sqrt(jnp.sum(jnp.sum(squares, axis=0, keepdims=True), axis=1, keepdims=True))
        factor = 1.0 / (norm + 1e-07)
        scale[...] = jnp.broadcast_to(math.sqrt(R) * jnp.sqrt(factor), (8, H))
        for i in range(4):
            for j in range(i + 1):
                product = jnp.dot(
                    gram[i * B : (i + 1) * B, :], gram[:, j * B : (j + 1) * B], preferred_element_type=jnp.float32
                )
                block = gram[i * B : (i + 1) * B, j * B : (j + 1) * B].astype(jnp.float32)
                block = (-4.775 * factor * block + 2.0315 * factor * factor * product).astype(jnp.bfloat16)
                poly[i * B : (i + 1) * B, j * B : (j + 1) * B] = block
                if i != j:
                    poly[j * B : (j + 1) * B, i * B : (i + 1) * B] = block.T

    x = x_ref[0]
    applied = jnp.dot(x, poly[...], preferred_element_type=jnp.float32)
    out_ref[0] = (scale[0:1, 0:1] * (3.4445 * x.astype(jnp.float32) + applied)).astype(jnp.bfloat16)


PART_A = jax.ShapeDtypeStruct((LARGE, B), jnp.bfloat16)
PART_B = jax.ShapeDtypeStruct((REST, B), jnp.bfloat16)
TILE = jax.ShapeDtypeStruct((8, H), jnp.float32)
SMEM = pl.BlockSpec(memory_space=pltpu.SMEM)
VMEM = pl.BlockSpec(memory_space=pltpu.VMEM)


def call(kernel, in_specs, outs, flops, nbytes, limit):
    return pl.pallas_call(
        kernel,
        out_shape=outs,
        in_specs=in_specs,
        out_specs=[VMEM] * len(outs),
        cost_estimate=pl.CostEstimate(flops=flops, bytes_accessed=nbytes, transcendentals=0),
        compiler_params=pltpu.CompilerParams(vmem_limit_bytes=limit << 20),
    )


def add_pieces(a, b):
    out = jax.ShapeDtypeStruct(a.shape, a.dtype)
    return call(add_kernel, [VMEM] * 2, [out], a.size, 6 * a.size, 6)(a, b)[0]


def finish(own, keep_a, keep_b, recv_a, recv_b, x, rows):
    step = 128
    return pl.pallas_call(
        final_kernel,
        grid=(rows // step,),
        out_shape=jax.ShapeDtypeStruct((1, rows, C), jnp.bfloat16),
        in_specs=[SMEM] + [VMEM] * 4 + [pl.BlockSpec((1, step, C), lambda i: (0, i, 0))],
        out_specs=pl.BlockSpec((1, step, C), lambda i: (0, i, 0)),
        scratch_shapes=[
            pltpu.VMEM((C, C), jnp.bfloat16),
            pltpu.VMEM((C, C), jnp.bfloat16),
            pltpu.VMEM((8, H), jnp.float32),
        ],
        cost_estimate=pl.CostEstimate(flops=4 * rows * C * C, bytes_accessed=4 * rows * C, transcendentals=0),
        compiler_params=pltpu.CompilerParams(vmem_limit_bytes=24 << 20),
    )(own, keep_a, keep_b, recv_a, recv_b, x)


PAIR = [(0, 1), (1, 0), (2, 3), (3, 2)]
CROSS = [(1, 2), (2, 1), (0, 3), (3, 0)]
DP = ("z", "y_hi", "x", "core")
Z, Y_HI, X, CORES = 12, 2, 4, 2


def over(line, axes):
    count = lax.axis_size(axes)
    parts = lax.all_to_all(jnp.broadcast_to(line, (count, H)), axes, 0, 0, tiled=True)
    return jnp.sum(parts, axis=0, keepdims=True)


def step(gradient):
    rows = gradient.shape[1]
    place = lax.axis_index("slab")
    own = jnp.where((place == 1) | (place == 2), 1, 0).astype(jnp.int32).reshape(1)
    work = rows * B * B * 2
    send_a, tile = call(first_kernel, [SMEM, VMEM], [PART_A, TILE], 3 * work, 2 * rows * C, 16)(own, gradient)
    got_a = lax.ppermute(send_a, "slab", PAIR)
    (send_b,) = call(second_kernel, [SMEM, VMEM], [PART_B], 2 * work, 2 * rows * C, 16)(own, gradient)
    got_b = lax.ppermute(send_b, "slab", PAIR)
    keep_a, keep_b = call(third_kernel, [SMEM, VMEM], [PART_A, PART_B], 5 * work, 2 * rows * C, 16)(own, gradient)
    half_a = add_pieces(keep_a, got_a)
    crossed_a = lax.ppermute(half_a, "slab", CROSS)
    total = over(tile[0:1], ("y_hi", "slab"))
    total = over(total, ("z",))
    half_b = add_pieces(keep_b, got_b)
    crossed_b = lax.ppermute(half_b, "slab", CROSS)
    whole_a = add_pieces(half_a, crossed_a)
    other_a = lax.ppermute(whole_a, "slab", PAIR)
    whole_b = add_pieces(half_b, crossed_b)
    other_b = lax.ppermute(whole_b, "slab", PAIR)
    total = over(total, ("x", "core"))
    update = finish(own, whole_a, whole_b, other_a, other_b, gradient, rows)
    entries = gradient.size * lax.axis_size(DP) * lax.axis_size("slab")
    return update, jnp.sqrt(total[0, 0] / entries)


def solution(mesh):
    named = Mesh(mesh.devices.reshape(Z, Y_HI, X, CORES, mesh.shape["slab"]), DP + ("slab",))
    placed = P(DP, "slab", None)
    return jax.shard_map(step, mesh=named, in_specs=(placed,), out_specs=(placed, P()), check_vma=False)
```

time: 75.9 us -> 113 us (1.49)
  the two profiles are of different devices: /device:TPU:56 before, /device:TPU:1 now
where the time goes in v3:
time: 113 us
  blocking collectives  51.6 us (46%)
  starting transfers between devices  33.3 us (29%)
  waiting for transfers between devices  14.8 us (13%)
  Pallas kernels  9.31 us (8%)
  between operations  2.02 us (2%)
  local copies, waits for them, and re-layouts  1.52 us (1%)
    all_to_all x3, blocking collectives, over(): lax.all_to_all(jnp.broadcast_to(line, (count, H)), axes, 0, 0, tiled=True)  51.6 us
    ppermute x1, starting transfers between devices, step(): crossed_a = lax.ppermute(half_a, 'slab', CROSS)  8.97 us
    ppermute x1, starting transfers between devices, step(): crossed_b = lax.ppermute(half_b, 'slab', CROSS)  8.62 us
    ppermute x1, starting transfers between devices, step(): other_a = lax.ppermute(whole_a, 'slab', PAIR)  7.89 us
    ppermute x1, waiting for transfers between devices, step(): crossed_b = lax.ppermute(half_b, 'slab', CROSS)  7.64 us
    pallas_call x1, Pallas kernels, finish(): pl.pallas_call(final_kernel, grid=(rows // step,), out_shape=jax.ShapeDty...  6.84 us
    ppermute x1, waiting for transfers between devices, step(): got_a = lax.ppermute(send_a, 'slab', PAIR)  4.23 us
    ppermute x1, starting transfers between devices, step(): got_a = lax.ppermute(send_a, 'slab', PAIR)  4.03 us
  transfers between devices with their start and end apart: 6, of which 3 were waited for; matrix products, arithmetic and copies ran while one was open for 0% of the time, Pallas kernels for 1%

profile of v3, /device:TPU:1, one launch (start us, length us, event | category | flops | bytes accessed | tf_op | source)
XLA Modules:
  0.0 112.7 jit_solution(8148692586636861771)
XLA Ops:
  0.6 0.0 copy-start
  0.7 1.5 %copy-done = bf16[1,896,1024]{2,1,0:T(8,128)(2,1)S(1)} copy-done((bf16[1,896,1024]{2,1,0:T(8,128)(2,1)S(1)}, bf16[1,896,1024]{2,1,0:T(8,128)(2,1)}, u32[]{:S(2)}) %copy-start) | copy-done | bytes 1835032
  2.1 0.8 shard_map.31
  2.9 4.0 %collective-permute-start = (bf16[784,256]{1,0:T(8,128)(2,1)S(1)}, bf16[784,256]{1,0:T(8,128)(2,1)S(1)}, u32[]{:S(2)}, u32[]{:S(2)}) collective-permute-start(bf16[784,256]{1,0:T(8,128)(2,1)S(1)} %get-tuple-element.7), channel_id=1, source_target_pairs={{0,1},{1,0},{2,3},{3,2},{4,5},{5,4},{6,7},{7,6},{8,9},{9,8},{10,11... | collective-permute-start | bytes 1204232 | tf_op jit(solution)/shard_map/ppermute | solution.py:211
  6.9 1.0 shard_map.30
  8.0 4.2 %collective-permute-done.b_ref = bf16[784,256]{1,0:T(8,128)(2,1)S(1)} collective-permute-done((bf16[784,256]{1,0:T(8,128)(2,1)S(1)}, bf16[784,256]{1,0:T(8,128)(2,1)S(1)}, u32[]{:S(2)}, u32[]{:S(2)}) %collective-permute-start) | collective-permute-done | bytes 401440 | tf_op jit(solution)/shard_map/ppermute | solution.py:211
  12.2 0.1 shard_map.32.a_ref
  12.3 0.0 copy-start.1
  12.3 9.0 %collective-permute-start.1 = (bf16[784,256]{1,0:T(8,128)(2,1)S(1)}, bf16[784,256]{1,0:T(8,128)(2,1)S(1)}, u32[]{:S(2)}, u32[]{:S(2)}) collective-permute-start(bf16[784,256]{1,0:T(8,128)(2,1)S(1)} %shard_map.32.a_ref), channel_id=1, source_target_pairs={{1,2},{2,1},{0,3},{3,0},{5,6},{6,5},{4,7},{7,4},{9,10},{10,9},{8,1... | collective-permute-start | bytes 1204232 | tf_op jit(solution)/shard_map/ppermute | solution.py:216
  21.3 0.4 shard_map.34
  21.7 1.9 %collective-permute-start.2 = (bf16[272,256]{1,0:T(8,128)(2,1)S(1)}, bf16[272,256]{1,0:T(8,128)(2,1)S(1)}, u32[]{:S(2)}, u32[]{:S(2)}) collective-permute-start(bf16[272,256]{1,0:T(8,128)(2,1)S(1)} %shard_map.34), channel_id=1, source_target_pairs={{0,1},{1,0},{2,3},{3,2},{4,5},{5,4},{6,7},{7,6},{8,9},{9,8},{10,11... | collective-permute-start | bytes 417800 | tf_op jit(solution)/shard_map/ppermute | solution.py:213
  23.7 3.0 %collective-permute-done.1.b_ref = bf16[784,256]{1,0:T(8,128)(2,1)S(1)} collective-permute-done((bf16[784,256]{1,0:T(8,128)(2,1)S(1)}, bf16[784,256]{1,0:T(8,128)(2,1)S(1)}, u32[]{:S(2)}, u32[]{:S(2)}) %collective-permute-start.1) | collective-permute-done | bytes 401440 | tf_op jit(solution)/shard_map/ppermute | solution.py:216
  26.6 0.1 shard_map.33.keep_a_ref
  26.7 7.9 %collective-permute-start.4 = (bf16[784,256]{1,0:T(8,128)(2,1)S(1)}, bf16[784,256]{1,0:T(8,128)(2,1)S(1)}, u32[]{:S(2)}, u32[]{:S(2)}) collective-permute-start(bf16[784,256]{1,0:T(8,128)(2,1)S(1)} %shard_map.33.keep_a_ref), channel_id=1, source_target_pairs={{0,1},{1,0},{2,3},{3,2},{4,5},{5,4},{6,7},{7,6},{8,9},{9,8},{10,11... | collective-permute-start | bytes 1204232 | tf_op jit(solution)/shard_map/ppermute | solution.py:222
  34.6 0.0 collective-permute-done.2.b_ref
  34.7 8.6 %collective-permute-start.3 = (bf16[272,256]{1,0:T(8,128)(2,1)S(1)}, bf16[272,256]{1,0:T(8,128)(2,1)S(1)}, u32[]{:S(2)}, u32[]{:S(2)}) collective-permute-start(bf16[272,256]{1,0:T(8,128)(2,1)S(1)} %shard_map.35.a_ref), channel_id=1, source_target_pairs={{1,2},{2,1},{0,3},{3,0},{5,6},{6,5},{4,7},{7,4},{9,10},{10,9},{8,1... | collective-permute-start | bytes 417800 | tf_op jit(solution)/shard_map/ppermute | solution.py:220
  43.3 7.6 %collective-permute-done.3.b_ref = bf16[272,256]{1,0:T(8,128)(2,1)S(1)} collective-permute-done((bf16[272,256]{1,0:T(8,128)(2,1)S(1)}, bf16[272,256]{1,0:T(8,128)(2,1)S(1)}, u32[]{:S(2)}, u32[]{:S(2)}) %collective-permute-start.3) | collective-permute-done | bytes 139296 | tf_op jit(solution)/shard_map/ppermute | solution.py:220
  51.0 1.9 %collective-permute-start.5 = (bf16[272,256]{1,0:T(8,128)(2,1)S(1)}, bf16[272,256]{1,0:T(8,128)(2,1)S(1)}, u32[]{:S(2)}, u32[]{:S(2)}) collective-permute-start(bf16[272,256]{1,0:T(8,128)(2,1)S(1)} %shard_map.36.keep_b_ref), channel_id=1, source_target_pairs={{0,1},{1,0},{2,3},{3,2},{4,5},{5,4},{6,7},{7,6},{8,9},{9,8},{10,11... | collective-permute-start | bytes 417800 | tf_op jit(solution)/shard_map/ppermute | solution.py:224
  52.9 13.5 %all_to_all.18 = f32[8,1,128]{2,1,0:T(1,128)S(1)} all-to-all(f32[8,1,128]{2,1,0:T(1,128)S(1)} %broadcast_in_dim.8), channel_id=1, replica_groups=mesh['z'=12,'y_hi'=2,'x'=4,'core'=2,'slab'=4] {'y_hi','slab'}, dimensions={0} | all-to-all | bytes 8192 | tf_op jit(solution)/shard_map/all_to_all | solution.py:201
  66.5 23.6 %all_to_all.19 = f32[12,1,128]{2,1,0:T(1,128)S(1)} all-to-all(f32[12,1,128]{2,1,0:T(1,128)S(1)} %broadcast_in_dim.9), channel_id=1, replica_groups=mesh['z'=12,'y_hi'=2,'x'=4,'core'=2,'slab'=4] {'z'}, dimensions={0} | all-to-all | bytes 12288 | tf_op jit(solution)/shard_map/all_to_all | solution.py:201
  90.1 14.5 %all_to_all.20 = f32[8,1,128]{2,1,0:T(1,128)S(1)} all-to-all(f32[8,1,128]{2,1,0:T(1,128)S(1)} %broadcast_in_dim.10), channel_id=1, replica_groups=mesh['z'=12,'y_hi'=2,'x'=4,'core'=2,'slab'=4] {'x','core'}, dimensions={0} | all-to-all | bytes 8192 | tf_op jit(solution)/shard_map/all_to_all | solution.py:201
  104.7 0.0 collective-permute-done.5.recv_b_ref
  104.7 0.0 collective-permute-done.4.recv_a_ref
  104.7 0.0 copy-done.1
  104.7 6.8 %shard_map.37 = bf16[1,896,1024]{2,1,0:T(8,128)(2,1)} custom-call(s32[1]{0:T(128)} %bitcast.own_ref, bf16[784,256]{1,0:T(8,128)(2,1)S(1)} %shard_map.33.keep_a_ref, bf16[272,256]{1,0:T(8,128)(2,1)S(1)} %shard_map.36.keep_b_ref, bf16[784,256]{1,0:T(8,128)(2,1)S(1)} %collective-permute-done.4.recv_a_ref, ...), custom_call_target="tpu_custom_call" | custom-call | flops 3758096384 | bytes 3670016 | tf_op jit(solution)/shard_map/pallas_call | solution.py:177
  (9 shorter events, 0.2 us)
Async XLA Ops:
  0.6 1.5 %copy-start = (bf16[1,896,1024]{2,1,0:T(8,128)(2,1)S(1)}, bf16[1,896,1024]{2,1,0:T(8,128)(2,1)}, u32[]{:S(2)}) copy-start(bf16[1,896,1024]{2,1,0:T(8,128)(2,1)} %x_ref.7) | copy-start | bytes 5505028
  2.9 9.3 %collective-permute-start = (bf16[784,256]{1,0:T(8,128)(2,1)S(1)}, bf16[784,256]{1,0:T(8,128)(2,1)S(1)}, u32[]{:S(2)}, u32[]{:S(2)}) collective-permute-start(bf16[784,256]{1,0:T(8,128)(2,1)S(1)} %get-tuple-element.7), channel_id=1, source_target_pairs={{0,1},{1,0},{2,3},{3,2},{4,5},{5,4},{6,7},{7,6},{8,9},{9,8},{10,11... | collective-permute-start | bytes 1204232 | tf_op jit(solution)/shard_map/ppermute | solution.py:211
  12.3 92.4 %copy-start.1 = (bf16[1,896,1024]{2,1,0:T(8,128)(2,1)S(1)}, bf16[1,896,1024]{2,1,0:T(8,128)(2,1)}, u32[]{:S(2)}) copy-start(bf16[1,896,1024]{2,1,0:T(8,128)(2,1)} %x_ref.7) | copy-start | bytes 5505028
  12.3 14.3 %collective-permute-start.1 = (bf16[784,256]{1,0:T(8,128)(2,1)S(1)}, bf16[784,256]{1,0:T(8,128)(2,1)S(1)}, u32[]{:S(2)}, u32[]{:S(2)}) collective-permute-start(bf16[784,256]{1,0:T(8,128)(2,1)S(1)} %shard_map.32.a_ref), channel_id=1, source_target_pairs={{1,2},{2,1},{0,3},{3,0},{5,6},{6,5},{4,7},{7,4},{9,10},{10,9},{8,1... | collective-permute-start | bytes 1204232 | tf_op jit(solution)/shard_map/ppermute | solution.py:216
  21.7 12.9 %collective-permute-start.2 = (bf16[272,256]{1,0:T(8,128)(2,1)S(1)}, bf16[272,256]{1,0:T(8,128)(2,1)S(1)}, u32[]{:S(2)}, u32[]{:S(2)}) collective-permute-start(bf16[272,256]{1,0:T(8,128)(2,1)S(1)} %shard_map.34), channel_id=1, source_target_pairs={{0,1},{1,0},{2,3},{3,2},{4,5},{5,4},{6,7},{7,6},{8,9},{9,8},{10,11... | collective-permute-start | bytes 417800 | tf_op jit(solution)/shard_map/ppermute | solution.py:213
  26.7 78.0 %collective-permute-start.4 = (bf16[784,256]{1,0:T(8,128)(2,1)S(1)}, bf16[784,256]{1,0:T(8,128)(2,1)S(1)}, u32[]{:S(2)}, u32[]{:S(2)}) collective-permute-start(bf16[784,256]{1,0:T(8,128)(2,1)S(1)} %shard_map.33.keep_a_ref), channel_id=1, source_target_pairs={{0,1},{1,0},{2,3},{3,2},{4,5},{5,4},{6,7},{7,6},{8,9},{9,8},{10,11... | collective-permute-start | bytes 1204232 | tf_op jit(solution)/shard_map/ppermute | solution.py:222
  34.7 16.3 %collective-permute-start.3 = (bf16[272,256]{1,0:T(8,128)(2,1)S(1)}, bf16[272,256]{1,0:T(8,128)(2,1)S(1)}, u32[]{:S(2)}, u32[]{:S(2)}) collective-permute-start(bf16[272,256]{1,0:T(8,128)(2,1)S(1)} %shard_map.35.a_ref), channel_id=1, source_target_pairs={{1,2},{2,1},{0,3},{3,0},{5,6},{6,5},{4,7},{7,4},{9,10},{10,9},{8,1... | collective-permute-start | bytes 417800 | tf_op jit(solution)/shard_map/ppermute | solution.py:220
  51.0 53.7 %collective-permute-start.5 = (bf16[272,256]{1,0:T(8,128)(2,1)S(1)}, bf16[272,256]{1,0:T(8,128)(2,1)S(1)}, u32[]{:S(2)}, u32[]{:S(2)}) collective-permute-start(bf16[272,256]{1,0:T(8,128)(2,1)S(1)} %shard_map.36.keep_b_ref), channel_id=1, source_target_pairs={{0,1},{1,0},{2,3},{3,2},{4,5},{5,4},{6,7},{7,6},{8,9},{9,8},{10,11... | collective-permute-start | bytes 417800 | tf_op jit(solution)/shard_map/ppermute | solution.py:224

commit v4 on v3

--- a/solution.py
+++ b/solution.py
@@ -88,65 +88,67 @@
     out_ref[...] = (a_ref[...].astype(jnp.float32) + b_ref[...].astype(jnp.float32)).astype(jnp.bfloat16)
 
 
-def final_kernel(own_ref, keep_a_ref, keep_b_ref, recv_a_ref, recv_b_ref, x_ref, out_ref, gram, poly, scale):
-    @pl.when(pl.program_id(0) == 0)
-    def _():
-        mine = own_ref[0] == 0
-        rows, cols = lower()
-        squares = jnp.zeros((H, B), jnp.float32)
-        for p in range(4):
-            low = p < 2
-
-            def get(small, start, size):
-                keep_ref, recv_ref = (keep_b_ref, recv_b_ref) if small else (keep_a_ref, recv_a_ref)
-                k, r = keep_ref[start : start + size, :], recv_ref[start : start + size, :]
-                return jnp.where(mine, k, r) if low else jnp.where(mine, r, k)
-
-            small = p % 2 == 1
-            top, base = (B + REST, 0) if small else (0, B)
-
-            def put(i, j, block):
-                gram[i : i + block.shape[0], j : j + block.shape[1]] = block
-                gram[j : j + block.shape[1], i : i + block.shape[0]] = block.T
-
-            block = get(False, top, B)
-            fi, fj = FULL[p]
-            put(fi * B, fj * B, block)
-            wide = block.astype(jnp.float32)
-            squares += 2.0 * (wide[:H] * wide[:H] + wide[H:] * wide[H:])
-            block = get(small, base, H)
-            hi, hj, part = HALF[p]
-            put(hi * B + part * H, hj * B, block)
-            wide = block.astype(jnp.float32)
-            squares += 2.0 * wide * wide
-            block = get(small, base + H, H)
-            put(p * B + H, p * B, block[:, :H])
-            fold = block[:, H:].astype(jnp.float32)
-            flip = fold.T
-            line = get(small, base + B, 16)[0:1, :H].astype(jnp.float32)
-            upper = jnp.where(rows < cols, flip, jnp.where(rows == cols, jnp.broadcast_to(line, (H, H)), fold))
-            second = jnp.where(rows > cols, flip, fold)
-            gram[p * B : p * B + H, p * B : p * B + H] = upper.astype(jnp.bfloat16)
-            gram[p * B + H : (p + 1) * B, p * B + H : (p + 1) * B] = second.astype(jnp.bfloat16)
-            wide = block[:, :H].astype(jnp.float32)
-            squares += jnp.concatenate([2.0 * wide * wide, upper * upper + second * second], axis=1)
-        norm = jnp.sqrt(jnp.sum(jnp.sum(squares, axis=0, keepdims=True), axis=1, keepdims=True))
-        factor = 1.0 / (norm + 1e-07)
-        scale[...] = jnp.broadcast_to(math.sqrt(R) * jnp.sqrt(factor), (8, H))
-        for i in range(4):
-            for j in range(i + 1):
-                product = jnp.dot(
-                    gram[i * B : (i + 1) * B, :], gram[:, j * B : (j + 1) * B], preferred_element_type=jnp.float32
-                )
-                block = gram[i * B : (i + 1) * B, j * B : (j + 1) * B].astype(jnp.float32)
-                block = (-4.775 * factor * block + 2.0315 * factor * factor * product).astype(jnp.bfloat16)
-                poly[i * B : (i + 1) * B, j * B : (j + 1) * B] = block
-                if i != j:
-                    poly[j * B : (j + 1) * B, i * B : (i + 1) * B] = block.T
-
-    x = x_ref[0]
-    applied = jnp.dot(x, poly[...], preferred_element_type=jnp.float32)
-    out_ref[0] = (scale[0:1, 0:1] * (3.4445 * x.astype(jnp.float32) + applied)).astype(jnp.bfloat16)
+def final_kernel(own_ref, keep_a_ref, keep_b_ref, recv_a_ref, recv_b_ref, x_ref, out_ref, gram, poly, done, sems):
+    mine = own_ref[0] == 0
+    rows, cols = lower()
+    squares = jnp.zeros((H, B), jnp.float32)
+    for p in range(4):
+        low = p < 2
+
+        def get(small, start, size):
+            keep_ref, recv_ref = (keep_b_ref, recv_b_ref) if small else (keep_a_ref, recv_a_ref)
+            k, r = keep_ref[start : start + size, :], recv_ref[start : start + size, :]
+            return jnp.where(mine, k, r) if low else jnp.where(mine, r, k)
+
+        small = p % 2 == 1
+        top, base = (B + REST, 0) if small else (0, B)
+
+        def put(i, j, block):
+            gram[i : i + block.shape[0], j : j + block.shape[1]] = block
+            gram[j : j + block.shape[1], i : i + block.shape[0]] = block.T
+
+        block = get(False, top, B)
+        fi, fj = FULL[p]
+        put(fi * B, fj * B, block)
+        wide = block.astype(jnp.float32)
+        squares += 2.0 * (wide[:H] * wide[:H] + wide[H:] * wide[H:])
+        block = get(small, base, H)
+        hi, hj, part = HALF[p]
+        put(hi * B + part * H, hj * B, block)
+        wide = block.astype(jnp.float32)
+        squares += 2.0 * wide * wide
+        block = get(small, base + H, H)
+        put(p * B + H, p * B, block[:, :H])
+        fold = block[:, H:].astype(jnp.float32)
+        flip = fold.T
+        line = get(small, base + B, 16)[0:1, :H].astype(jnp.float32)
+        upper = jnp.where(rows < cols, flip, jnp.where(rows == cols, jnp.broadcast_to(line, (H, H)), fold))
+        second = jnp.where(rows > cols, flip, fold)
+        gram[p * B : p * B + H, p * B : p * B + H] = upper.astype(jnp.bfloat16)
+        gram[p * B + H : (p + 1) * B, p * B + H : (p + 1) * B] = second.astype(jnp.bfloat16)
+        wide = block[:, :H].astype(jnp.float32)
+        squares += jnp.concatenate([2.0 * wide * wide, upper * upper + second * second], axis=1)
+    norm = jnp.sqrt(jnp.sum(jnp.sum(squares, axis=0, keepdims=True), axis=1, keepdims=True))
+    factor = 1.0 / (norm + 1e-07)
+    for j in range(4):
+        cols = slice(j * B, (j + 1) * B)
+        product = jnp.dot(gram[j * B :, :], gram[:, cols], preferred_element_type=jnp.float32)
+        block = gram[j * B :, cols].astype(jnp.float32)
+        block = (-4.775 * factor * block + 2.0315 * factor * factor * product).astype(jnp.bfloat16)
+        poly[j * B :, cols] = block
+        for i in range(j + 1, 4):
+            poly[cols, i * B : (i + 1) * B] = block[(i - j) * B : (i - j + 1) * B, :].T
+
+    scale = math.sqrt(R) * jnp.sqrt(factor)
+    copies = []
+    for j in range(4):
+        cols = slice(j * B, (j + 1) * B)
+        applied = jnp.dot(x_ref[0], poly[:, cols], preferred_element_type=jnp.float32)
+        done[0, :, cols] = (scale * (3.4445 * x_ref[0, :, cols].astype(jnp.float32) + applied)).astype(jnp.bfloat16)
+        copies.append(pltpu.make_async_copy(done.at[:, :, cols], out_ref.at[:, :, cols], sems.at[j]))
+        copies[-1].start()
+    for copy in copies:
+        copy.wait()
 
 
 PART_A = jax.ShapeDtypeStruct((LARGE, B), jnp.bfloat16)
@@ -173,20 +175,19 @@
 
 
 def finish(own, keep_a, keep_b, recv_a, recv_b, x, rows):
-    step = 128
     return pl.pallas_call(
         final_kernel,
-        grid=(rows // step,),
         out_shape=jax.ShapeDtypeStruct((1, rows, C), jnp.bfloat16),
-        in_specs=[SMEM] + [VMEM] * 4 + [pl.BlockSpec((1, step, C), lambda i: (0, i, 0))],
-        out_specs=pl.BlockSpec((1, step, C), lambda i: (0, i, 0)),
+        in_specs=[SMEM] + [VMEM] * 5,
+        out_specs=pl.BlockSpec(memory_space=pl.ANY),
         scratch_shapes=[
             pltpu.VMEM((C, C), jnp.bfloat16),
             pltpu.VMEM((C, C), jnp.bfloat16),
-            pltpu.VMEM((8, H), jnp.float32),
+            pltpu.VMEM((1, rows, C), jnp.bfloat16),
+            pltpu.SemaphoreType.DMA((4,)),
         ],
         cost_estimate=pl.CostEstimate(flops=4 * rows * C * C, bytes_accessed=4 * rows * C, transcendentals=0),
-        compiler_params=pltpu.CompilerParams(vmem_limit_bytes=24 << 20),
+        compiler_params=pltpu.CompilerParams(vmem_limit_bytes=32 << 20),
     )(own, keep_a, keep_b, recv_a, recv_b, x)
 
 
@@ -198,7 +199,8 @@
 
 def over(line, axes):
     count = lax.axis_size(axes)
-    parts = lax.all_to_all(jnp.broadcast_to(line, (count, H)), axes, 0, 0, tiled=True)
+    lines = line if line.shape[0] == count else jnp.broadcast_to(line, (count, H))
+    parts = lax.all_to_all(lines, axes, 0, 0, tiled=True)
     return jnp.sum(parts, axis=0, keepdims=True)
 
 
@@ -214,7 +216,7 @@
     keep_a, keep_b = call(third_kernel, [SMEM, VMEM], [PART_A, PART_B], 5 * work, 2 * rows * C, 16)(own, gradient)
     half_a = add_pieces(keep_a, got_a)
     crossed_a = lax.ppermute(half_a, "slab", CROSS)
-    total = over(tile[0:1], ("y_hi", "slab"))
+    total = over(tile, ("y_hi", "slab"))
     total = over(total, ("z",))
     half_b = add_pieces(keep_b, got_b)
     crossed_b = lax.ppermute(half_b, "slab", CROSS)

time: 113 us -> 111 us (0.982)
  Pallas kernels: 9.31 us -> 7.48 us
    pallas_call x1, Pallas kernels: 6.84 us -> 5.02 us  [finish(): pl.pallas_call(final_kernel, out_shape=jax.ShapeDtypeStruct((1, rows, C),...]
where the time goes in v4:
time: 111 us
  blocking collectives  51.6 us (46%)
  starting transfers between devices  33.3 us (30%)
  waiting for transfers between devices  14.8 us (13%)
  Pallas kernels  7.48 us (7%)
  between operations  2 us (2%)
  local copies, waits for them, and re-layouts  1.52 us (1%)
    all_to_all x3, blocking collectives, over(): parts = lax.all_to_all(lines, axes, 0, 0, tiled=True)  51.6 us
    ppermute x1, starting transfers between devices, step(): crossed_a = lax.ppermute(half_a, 'slab', CROSS)  8.97 us
    ppermute x1, starting transfers between devices, step(): crossed_b = lax.ppermute(half_b, 'slab', CROSS)  8.62 us
    ppermute x1, starting transfers between devices, step(): other_a = lax.ppermute(whole_a, 'slab', PAIR)  7.89 us
    ppermute x1, waiting for transfers between devices, step(): crossed_b = lax.ppermute(half_b, 'slab', CROSS)  7.64 us
    pallas_call x1, Pallas kernels, finish(): pl.pallas_call(final_kernel, out_shape=jax.ShapeDtypeStruct((1, rows, C),...  5.02 us
    ppermute x1, waiting for transfers between devices, step(): got_a = lax.ppermute(send_a, 'slab', PAIR)  4.23 us
    ppermute x1, starting transfers between devices, step(): got_a = lax.ppermute(send_a, 'slab', PAIR)  4.03 us
  transfers between devices with their start and end apart: 6, of which 3 were waited for; matrix products, arithmetic and copies ran while one was open for 0% of the time, Pallas kernels for 1%

profile of v4, /device:TPU:1, one launch (start us, length us, event | category | flops | bytes accessed | tf_op | source)
XLA Modules:
  0.0 110.9 jit_solution(3375410439552946519)
XLA Ops:
  0.6 0.0 copy-start
  0.7 1.5 %copy-done = bf16[1,896,1024]{2,1,0:T(8,128)(2,1)S(1)} copy-done((bf16[1,896,1024]{2,1,0:T(8,128)(2,1)S(1)}, bf16[1,896,1024]{2,1,0:T(8,128)(2,1)}, u32[]{:S(2)}) %copy-start) | copy-done | bytes 1835032
  2.1 0.8 shard_map.31
  2.9 4.0 %collective-permute-start = (bf16[784,256]{1,0:T(8,128)(2,1)S(1)}, bf16[784,256]{1,0:T(8,128)(2,1)S(1)}, u32[]{:S(2)}, u32[]{:S(2)}) collective-permute-start(bf16[784,256]{1,0:T(8,128)(2,1)S(1)} %get-tuple-element.7), channel_id=1, source_target_pairs={{0,1},{1,0},{2,3},{3,2},{4,5},{5,4},{6,7},{7,6},{8,9},{9,8},{10,11... | collective-permute-start | bytes 1204232 | tf_op jit(solution)/shard_map/ppermute | solution.py:213
  6.9 1.0 shard_map.30
  8.0 4.2 %collective-permute-done.b_ref = bf16[784,256]{1,0:T(8,128)(2,1)S(1)} collective-permute-done((bf16[784,256]{1,0:T(8,128)(2,1)S(1)}, bf16[784,256]{1,0:T(8,128)(2,1)S(1)}, u32[]{:S(2)}, u32[]{:S(2)}) %collective-permute-start) | collective-permute-done | bytes 401440 | tf_op jit(solution)/shard_map/ppermute | solution.py:213
  12.2 0.1 shard_map.32.a_ref
  12.3 0.0 copy-start.1
  12.3 9.0 %collective-permute-start.1 = (bf16[784,256]{1,0:T(8,128)(2,1)S(1)}, bf16[784,256]{1,0:T(8,128)(2,1)S(1)}, u32[]{:S(2)}, u32[]{:S(2)}) collective-permute-start(bf16[784,256]{1,0:T(8,128)(2,1)S(1)} %shard_map.32.a_ref), channel_id=1, source_target_pairs={{1,2},{2,1},{0,3},{3,0},{5,6},{6,5},{4,7},{7,4},{9,10},{10,9},{8,1... | collective-permute-start | bytes 1204232 | tf_op jit(solution)/shard_map/ppermute | solution.py:218
  21.3 0.4 shard_map.34
  21.7 1.9 %collective-permute-start.2 = (bf16[272,256]{1,0:T(8,128)(2,1)S(1)}, bf16[272,256]{1,0:T(8,128)(2,1)S(1)}, u32[]{:S(2)}, u32[]{:S(2)}) collective-permute-start(bf16[272,256]{1,0:T(8,128)(2,1)S(1)} %shard_map.34), channel_id=1, source_target_pairs={{0,1},{1,0},{2,3},{3,2},{4,5},{5,4},{6,7},{7,6},{8,9},{9,8},{10,11... | collective-permute-start | bytes 417800 | tf_op jit(solution)/shard_map/ppermute | solution.py:215
  23.7 3.0 %collective-permute-done.1.b_ref = bf16[784,256]{1,0:T(8,128)(2,1)S(1)} collective-permute-done((bf16[784,256]{1,0:T(8,128)(2,1)S(1)}, bf16[784,256]{1,0:T(8,128)(2,1)S(1)}, u32[]{:S(2)}, u32[]{:S(2)}) %collective-permute-start.1) | collective-permute-done | bytes 401440 | tf_op jit(solution)/shard_map/ppermute | solution.py:218
  26.6 0.1 shard_map.33.keep_a_ref
  26.7 7.9 %collective-permute-start.4 = (bf16[784,256]{1,0:T(8,128)(2,1)S(1)}, bf16[784,256]{1,0:T(8,128)(2,1)S(1)}, u32[]{:S(2)}, u32[]{:S(2)}) collective-permute-start(bf16[784,256]{1,0:T(8,128)(2,1)S(1)} %shard_map.33.keep_a_ref), channel_id=1, source_target_pairs={{0,1},{1,0},{2,3},{3,2},{4,5},{5,4},{6,7},{7,6},{8,9},{9,8},{10,11... | collective-permute-start | bytes 1204232 | tf_op jit(solution)/shard_map/ppermute | solution.py:224
  34.6 0.0 collective-permute-done.2.b_ref
  34.7 8.6 %collective-permute-start.3 = (bf16[272,256]{1,0:T(8,128)(2,1)S(1)}, bf16[272,256]{1,0:T(8,128)(2,1)S(1)}, u32[]{:S(2)}, u32[]{:S(2)}) collective-permute-start(bf16[272,256]{1,0:T(8,128)(2,1)S(1)} %shard_map.35.a_ref), channel_id=1, source_target_pairs={{1,2},{2,1},{0,3},{3,0},{5,6},{6,5},{4,7},{7,4},{9,10},{10,9},{8,1... | collective-permute-start | bytes 417800 | tf_op jit(solution)/shard_map/ppermute | solution.py:222
  43.3 7.6 %collective-permute-done.3.b_ref = bf16[272,256]{1,0:T(8,128)(2,1)S(1)} collective-permute-done((bf16[272,256]{1,0:T(8,128)(2,1)S(1)}, bf16[272,256]{1,0:T(8,128)(2,1)S(1)}, u32[]{:S(2)}, u32[]{:S(2)}) %collective-permute-start.3) | collective-permute-done | bytes 139296 | tf_op jit(solution)/shard_map/ppermute | solution.py:222
  51.0 1.9 %collective-permute-start.5 = (bf16[272,256]{1,0:T(8,128)(2,1)S(1)}, bf16[272,256]{1,0:T(8,128)(2,1)S(1)}, u32[]{:S(2)}, u32[]{:S(2)}) collective-permute-start(bf16[272,256]{1,0:T(8,128)(2,1)S(1)} %shard_map.36.keep_b_ref), channel_id=1, source_target_pairs={{0,1},{1,0},{2,3},{3,2},{4,5},{5,4},{6,7},{7,6},{8,9},{9,8},{10,11... | collective-permute-start | bytes 417800 | tf_op jit(solution)/shard_map/ppermute | solution.py:226
  52.9 13.5 %all_to_all.21 = f32[8,1,128]{2,1,0:T(1,128)S(1)} all-to-all(f32[8,1,128]{2,1,0:T(1,128)S(1)} %bitcast.8), channel_id=1, replica_groups=mesh['z'=12,'y_hi'=2,'x'=4,'core'=2,'slab'=4] {'y_hi','slab'}, dimensions={0} | all-to-all | bytes 8192 | tf_op jit(solution)/shard_map/all_to_all | solution.py:203
  66.5 23.6 %all_to_all.22 = f32[12,1,128]{2,1,0:T(1,128)S(1)} all-to-all(f32[12,1,128]{2,1,0:T(1,128)S(1)} %broadcast_in_dim.6), channel_id=1, replica_groups=mesh['z'=12,'y_hi'=2,'x'=4,'core'=2,'slab'=4] {'z'}, dimensions={0} | all-to-all | bytes 12288 | tf_op jit(solution)/shard_map/all_to_all | solution.py:203
  90.1 14.5 %all_to_all.23 = f32[8,1,128]{2,1,0:T(1,128)S(1)} all-to-all(f32[8,1,128]{2,1,0:T(1,128)S(1)} %broadcast_in_dim.7), channel_id=1, replica_groups=mesh['z'=12,'y_hi'=2,'x'=4,'core'=2,'slab'=4] {'x','core'}, dimensions={0} | all-to-all | bytes 8192 | tf_op jit(solution)/shard_map/all_to_all | solution.py:203
  104.7 0.0 collective-permute-done.5.recv_b_ref
  104.7 0.0 collective-permute-done.4.recv_a_ref
  104.7 0.0 copy-done.1
  104.7 5.0 %shard_map.37 = bf16[1,896,1024]{2,1,0:T(8,128)(2,1)} custom-call(s32[1]{0:T(128)} %bitcast.own_ref, bf16[784,256]{1,0:T(8,128)(2,1)S(1)} %shard_map.33.keep_a_ref, bf16[272,256]{1,0:T(8,128)(2,1)S(1)} %shard_map.36.keep_b_ref, bf16[784,256]{1,0:T(8,128)(2,1)S(1)} %collective-permute-done.4.recv_a_ref, ...), custom_call_target="tpu_custom_call" | custom-call | flops 3758096384 | bytes 3670016 | tf_op jit(solution)/shard_map/pallas_call | solution.py:178
  (7 shorter events, 0.2 us)
Async XLA Ops:
  0.6 1.5 %copy-start = (bf16[1,896,1024]{2,1,0:T(8,128)(2,1)S(1)}, bf16[1,896,1024]{2,1,0:T(8,128)(2,1)}, u32[]{:S(2)}) copy-start(bf16[1,896,1024]{2,1,0:T(8,128)(2,1)} %x_ref.7) | copy-start | bytes 5505028
  2.9 9.3 %collective-permute-start = (bf16[784,256]{1,0:T(8,128)(2,1)S(1)}, bf16[784,256]{1,0:T(8,128)(2,1)S(1)}, u32[]{:S(2)}, u32[]{:S(2)}) collective-permute-start(bf16[784,256]{1,0:T(8,128)(2,1)S(1)} %get-tuple-element.7), channel_id=1, source_target_pairs={{0,1},{1,0},{2,3},{3,2},{4,5},{5,4},{6,7},{7,6},{8,9},{9,8},{10,11... | collective-permute-start | bytes 1204232 | tf_op jit(solution)/shard_map/ppermute | solution.py:213
  12.3 92.4 %copy-start.1 = (bf16[1,896,1024]{2,1,0:T(8,128)(2,1)S(1)}, bf16[1,896,1024]{2,1,0:T(8,128)(2,1)}, u32[]{:S(2)}) copy-start(bf16[1,896,1024]{2,1,0:T(8,128)(2,1)} %x_ref.7) | copy-start | bytes 5505028
  12.3 14.3 %collective-permute-start.1 = (bf16[784,256]{1,0:T(8,128)(2,1)S(1)}, bf16[784,256]{1,0:T(8,128)(2,1)S(1)}, u32[]{:S(2)}, u32[]{:S(2)}) collective-permute-start(bf16[784,256]{1,0:T(8,128)(2,1)S(1)} %shard_map.32.a_ref), channel_id=1, source_target_pairs={{1,2},{2,1},{0,3},{3,0},{5,6},{6,5},{4,7},{7,4},{9,10},{10,9},{8,1... | collective-permute-start | bytes 1204232 | tf_op jit(solution)/shard_map/ppermute | solution.py:218
  21.7 12.9 %collective-permute-start.2 = (bf16[272,256]{1,0:T(8,128)(2,1)S(1)}, bf16[272,256]{1,0:T(8,128)(2,1)S(1)}, u32[]{:S(2)}, u32[]{:S(2)}) collective-permute-start(bf16[272,256]{1,0:T(8,128)(2,1)S(1)} %shard_map.34), channel_id=1, source_target_pairs={{0,1},{1,0},{2,3},{3,2},{4,5},{5,4},{6,7},{7,6},{8,9},{9,8},{10,11... | collective-permute-start | bytes 417800 | tf_op jit(solution)/shard_map/ppermute | solution.py:215
  26.7 78.0 %collective-permute-start.4 = (bf16[784,256]{1,0:T(8,128)(2,1)S(1)}, bf16[784,256]{1,0:T(8,128)(2,1)S(1)}, u32[]{:S(2)}, u32[]{:S(2)}) collective-permute-start(bf16[784,256]{1,0:T(8,128)(2,1)S(1)} %shard_map.33.keep_a_ref), channel_id=1, source_target_pairs={{0,1},{1,0},{2,3},{3,2},{4,5},{5,4},{6,7},{7,6},{8,9},{9,8},{10,11... | collective-permute-start | bytes 1204232 | tf_op jit(solution)/shard_map/ppermute | solution.py:224
  34.7 16.3 %collective-permute-start.3 = (bf16[272,256]{1,0:T(8,128)(2,1)S(1)}, bf16[272,256]{1,0:T(8,128)(2,1)S(1)}, u32[]{:S(2)}, u32[]{:S(2)}) collective-permute-start(bf16[272,256]{1,0:T(8,128)(2,1)S(1)} %shard_map.35.a_ref), channel_id=1, source_target_pairs={{1,2},{2,1},{0,3},{3,0},{5,6},{6,5},{4,7},{7,4},{9,10},{10,9},{8,1... | collective-permute-start | bytes 417800 | tf_op jit(solution)/shard_map/ppermute | solution.py:222
  51.0 53.7 %collective-permute-start.5 = (bf16[272,256]{1,0:T(8,128)(2,1)S(1)}, bf16[272,256]{1,0:T(8,128)(2,1)S(1)}, u32[]{:S(2)}, u32[]{:S(2)}) collective-permute-start(bf16[272,256]{1,0:T(8,128)(2,1)S(1)} %shard_map.36.keep_b_ref), channel_id=1, source_target_pairs={{0,1},{1,0},{2,3},{3,2},{4,5},{5,4},{6,7},{7,6},{8,9},{9,8},{10,11... | collective-permute-start | bytes 417800 | tf_op jit(solution)/shard_map/ppermute | solution.py:226

commit v5 on v4

--- a/solution.py
+++ b/solution.py
@@ -1,3 +1,4 @@
+import functools
 import math
 
 import jax
@@ -67,15 +68,15 @@
     whole_block(x_ref, 2 * half + 1, out_ref, B + REST)
 
 
-def first_kernel(own_ref, x_ref, out_ref, sum_ref):
+def first_kernel(own_ref, x_ref, out_ref):
+    large_part(x_ref, 1 - own_ref[0], out_ref)
+
+
+def second_kernel(own_ref, x_ref, out_ref, sum_ref):
     wide = x_ref[0].astype(jnp.float32)
     squares = jnp.sum(wide * wide, axis=0, keepdims=True)
     total = jnp.sum(squares, axis=1, keepdims=True)
     sum_ref[...] = jnp.broadcast_to(total, (8, H))
-    large_part(x_ref, 1 - own_ref[0], out_ref)
-
-
-def second_kernel(own_ref, x_ref, out_ref):
     rest(x_ref, 2 * (1 - own_ref[0]) + 1, out_ref, 0)
 
 
@@ -197,11 +198,19 @@
 Z, Y_HI, X, CORES = 12, 2, 4, 2
 
 
-def over(line, axes):
+def root_kernel(entries, parts_ref, out_ref):
+    total = jnp.sum(parts_ref[...], axis=0, keepdims=True)
+    out_ref[...] = jnp.sqrt(total[:, 0:1] / entries)
+
+
+def parts_over(line, axes):
     count = lax.axis_size(axes)
     lines = line if line.shape[0] == count else jnp.broadcast_to(line, (count, H))
-    parts = lax.all_to_all(lines, axes, 0, 0, tiled=True)
-    return jnp.sum(parts, axis=0, keepdims=True)
+    return lax.all_to_all(lines, axes, 0, 0, tiled=True)
+
+
+def over(line, axes):
+    return jnp.sum(parts_over(line, axes), axis=0, keepdims=True)
 
 
 def step(gradient):
@@ -209,9 +218,9 @@
     place = lax.axis_index("slab")
     own = jnp.where((place == 1) | (place == 2), 1, 0).astype(jnp.int32).reshape(1)
     work = rows * B * B * 2
-    send_a, tile = call(first_kernel, [SMEM, VMEM], [PART_A, TILE], 3 * work, 2 * rows * C, 16)(own, gradient)
+    (send_a,) = call(first_kernel, [SMEM, VMEM], [PART_A], 3 * work, 2 * rows * C, 16)(own, gradient)
     got_a = lax.ppermute(send_a, "slab", PAIR)
-    (send_b,) = call(second_kernel, [SMEM, VMEM], [PART_B], 2 * work, 2 * rows * C, 16)(own, gradient)
+    send_b, tile = call(second_kernel, [SMEM, VMEM], [PART_B, TILE], 2 * work, 2 * rows * C, 16)(own, gradient)
     got_b = lax.ppermute(send_b, "slab", PAIR)
     keep_a, keep_b = call(third_kernel, [SMEM, VMEM], [PART_A, PART_B], 5 * work, 2 * rows * C, 16)(own, gradient)
     half_a = add_pieces(keep_a, got_a)
@@ -224,10 +233,12 @@
     other_a = lax.ppermute(whole_a, "slab", PAIR)
     whole_b = add_pieces(half_b, crossed_b)
     other_b = lax.ppermute(whole_b, "slab", PAIR)
-    total = over(total, ("x", "core"))
+    parts = parts_over(total, ("x", "core"))
     update = finish(own, whole_a, whole_b, other_a, other_b, gradient, rows)
     entries = gradient.size * lax.axis_size(DP) * lax.axis_size("slab")
-    return update, jnp.sqrt(total[0, 0] / entries)
+    root = functools.partial(root_kernel, float(entries))
+    (rms,) = call(root, [VMEM], [jax.ShapeDtypeStruct((1, 1), jnp.float32)], 8 * H, 32 * H, 1)(parts)
+    return update, rms.reshape(())
 
 
 def solution(mesh):

time: 111 us -> 111 us (level)
  between operations: 2 us -> 0.76 us
  transfers between devices with their start and end apart: 6 -> 6, of which waited for: 3 -> 3; matrix products, arithmetic and copies ran while one was open for 0% -> 0% of each run, Pallas kernels for 1% -> 2%
where the time goes in v5:
time: 111 us; the launch traced here: 110 us
  blocking collectives  51.6 us (46%)
  starting transfers between devices  33.3 us (30%)
  waiting for transfers between devices  14.8 us (13%)
  Pallas kernels  8.02 us (7%)
  local copies, waits for them, and re-layouts  1.52 us (1%)
    all_to_all x3, blocking collectives, parts_over(): return lax.all_to_all(lines, axes, 0, 0, tiled=True)  51.6 us
    ppermute x1, starting transfers between devices, step(): crossed_a = lax.ppermute(half_a, 'slab', CROSS)  8.97 us
    ppermute x1, starting transfers between devices, step(): crossed_b = lax.ppermute(half_b, 'slab', CROSS)  8.61 us
    ppermute x1, starting transfers between devices, step(): other_a = lax.ppermute(whole_a, 'slab', PAIR)  7.89 us
    ppermute x1, waiting for transfers between devices, step(): crossed_b = lax.ppermute(half_b, 'slab', CROSS)  7.64 us
    pallas_call x1, Pallas kernels, finish(): pl.pallas_call(final_kernel, out_shape=jax.ShapeDtypeStruct((1, rows, C),...  5.02 us
    ppermute x1, waiting for transfers between devices, step(): got_a = lax.ppermute(send_a, 'slab', PAIR)  4.23 us
    ppermute x1, starting transfers between devices, step(): got_a = lax.ppermute(send_a, 'slab', PAIR)  4.02 us
  transfers between devices with their start and end apart: 6, of which 3 were waited for; matrix products, arithmetic and copies ran while one was open for 0% of the time, Pallas kernels for 2%

profile of v5, /device:TPU:1, one launch (start us, length us, event | category | flops | bytes accessed | tf_op | source)
XLA Modules:
  0.0 110.1 jit_solution(15249540777830761214)
XLA Ops:
  0.6 0.0 copy-start
  0.7 1.5 %copy-done = bf16[1,896,1024]{2,1,0:T(8,128)(2,1)S(1)} copy-done((bf16[1,896,1024]{2,1,0:T(8,128)(2,1)S(1)}, bf16[1,896,1024]{2,1,0:T(8,128)(2,1)}, u32[]{:S(2)}) %copy-start) | copy-done | bytes 1835032
  2.1 0.8 shard_map.31
  2.9 4.0 %collective-permute-start = (bf16[784,256]{1,0:T(8,128)(2,1)S(1)}, bf16[784,256]{1,0:T(8,128)(2,1)S(1)}, u32[]{:S(2)}, u32[]{:S(2)}) collective-permute-start(bf16[784,256]{1,0:T(8,128)(2,1)S(1)} %shard_map.31), channel_id=1, source_target_pairs={{0,1},{1,0},{2,3},{3,2},{4,5},{5,4},{6,7},{7,6},{8,9},{9,8},{10,11... | collective-permute-start | bytes 1204232 | tf_op jit(solution)/shard_map/ppermute | solution.py:222
  6.9 1.0 shard_map.30
  8.0 4.2 %collective-permute-done.b_ref = bf16[784,256]{1,0:T(8,128)(2,1)S(1)} collective-permute-done((bf16[784,256]{1,0:T(8,128)(2,1)S(1)}, bf16[784,256]{1,0:T(8,128)(2,1)S(1)}, u32[]{:S(2)}, u32[]{:S(2)}) %collective-permute-start) | collective-permute-done | bytes 401440 | tf_op jit(solution)/shard_map/ppermute | solution.py:222
  12.2 0.1 shard_map.32.a_ref
  12.3 0.0 copy-start.1
  12.3 9.0 %collective-permute-start.1 = (bf16[784,256]{1,0:T(8,128)(2,1)S(1)}, bf16[784,256]{1,0:T(8,128)(2,1)S(1)}, u32[]{:S(2)}, u32[]{:S(2)}) collective-permute-start(bf16[784,256]{1,0:T(8,128)(2,1)S(1)} %shard_map.32.a_ref), channel_id=1, source_target_pairs={{1,2},{2,1},{0,3},{3,0},{5,6},{6,5},{4,7},{7,4},{9,10},{10,9},{8,1... | collective-permute-start | bytes 1204232 | tf_op jit(solution)/shard_map/ppermute | solution.py:227
  21.3 0.4 shard_map.34
  21.7 1.9 %collective-permute-start.2 = (bf16[272,256]{1,0:T(8,128)(2,1)S(1)}, bf16[272,256]{1,0:T(8,128)(2,1)S(1)}, u32[]{:S(2)}, u32[]{:S(2)}) collective-permute-start(bf16[272,256]{1,0:T(8,128)(2,1)S(1)} %get-tuple-element.8), channel_id=1, source_target_pairs={{0,1},{1,0},{2,3},{3,2},{4,5},{5,4},{6,7},{7,6},{8,9},{9,8},{10,11... | collective-permute-start | bytes 417800 | tf_op jit(solution)/shard_map/ppermute | solution.py:224
  23.7 3.0 %collective-permute-done.1.b_ref = bf16[784,256]{1,0:T(8,128)(2,1)S(1)} collective-permute-done((bf16[784,256]{1,0:T(8,128)(2,1)S(1)}, bf16[784,256]{1,0:T(8,128)(2,1)S(1)}, u32[]{:S(2)}, u32[]{:S(2)}) %collective-permute-start.1) | collective-permute-done | bytes 401440 | tf_op jit(solution)/shard_map/ppermute | solution.py:227
  26.6 0.1 shard_map.33.keep_a_ref
  26.7 7.9 %collective-permute-start.4 = (bf16[784,256]{1,0:T(8,128)(2,1)S(1)}, bf16[784,256]{1,0:T(8,128)(2,1)S(1)}, u32[]{:S(2)}, u32[]{:S(2)}) collective-permute-start(bf16[784,256]{1,0:T(8,128)(2,1)S(1)} %shard_map.33.keep_a_ref), channel_id=1, source_target_pairs={{0,1},{1,0},{2,3},{3,2},{4,5},{5,4},{6,7},{7,6},{8,9},{9,8},{10,11... | collective-permute-start | bytes 1204232 | tf_op jit(solution)/shard_map/ppermute | solution.py:233
  34.6 0.0 collective-permute-done.2.b_ref
  34.7 8.6 %collective-permute-start.3 = (bf16[272,256]{1,0:T(8,128)(2,1)S(1)}, bf16[272,256]{1,0:T(8,128)(2,1)S(1)}, u32[]{:S(2)}, u32[]{:S(2)}) collective-permute-start(bf16[272,256]{1,0:T(8,128)(2,1)S(1)} %shard_map.35.a_ref), channel_id=1, source_target_pairs={{1,2},{2,1},{0,3},{3,0},{5,6},{6,5},{4,7},{7,4},{9,10},{10,9},{8,1... | collective-permute-start | bytes 417800 | tf_op jit(solution)/shard_map/ppermute | solution.py:231
  43.3 7.6 %collective-permute-done.3.b_ref = bf16[272,256]{1,0:T(8,128)(2,1)S(1)} collective-permute-done((bf16[272,256]{1,0:T(8,128)(2,1)S(1)}, bf16[272,256]{1,0:T(8,128)(2,1)S(1)}, u32[]{:S(2)}, u32[]{:S(2)}) %collective-permute-start.3) | collective-permute-done | bytes 139296 | tf_op jit(solution)/shard_map/ppermute | solution.py:231
  51.0 1.9 %collective-permute-start.5 = (bf16[272,256]{1,0:T(8,128)(2,1)S(1)}, bf16[272,256]{1,0:T(8,128)(2,1)S(1)}, u32[]{:S(2)}, u32[]{:S(2)}) collective-permute-start(bf16[272,256]{1,0:T(8,128)(2,1)S(1)} %shard_map.36.keep_b_ref), channel_id=1, source_target_pairs={{0,1},{1,0},{2,3},{3,2},{4,5},{5,4},{6,7},{7,6},{8,9},{9,8},{10,11... | collective-permute-start | bytes 417800 | tf_op jit(solution)/shard_map/ppermute | solution.py:235
  52.9 13.5 %all_to_all.23 = f32[8,1,128]{2,1,0:T(1,128)S(1)} all-to-all(f32[8,1,128]{2,1,0:T(1,128)S(1)} %bitcast.7), channel_id=1, replica_groups=mesh['z'=12,'y_hi'=2,'x'=4,'core'=2,'slab'=4] {'y_hi','slab'}, dimensions={0} | all-to-all | bytes 8192 | tf_op jit(solution)/shard_map/all_to_all | solution.py:209
  66.4 23.6 %all_to_all.24 = f32[12,1,128]{2,1,0:T(1,128)S(1)} all-to-all(f32[12,1,128]{2,1,0:T(1,128)S(1)} %broadcast_in_dim.4), channel_id=1, replica_groups=mesh['z'=12,'y_hi'=2,'x'=4,'core'=2,'slab'=4] {'z'}, dimensions={0} | all-to-all | bytes 12288 | tf_op jit(solution)/shard_map/all_to_all | solution.py:209
  90.1 14.5 %all_to_all.25 = f32[8,1,128]{2,1,0:T(1,128)S(1)} all-to-all(f32[8,1,128]{2,1,0:T(1,128)S(1)} %broadcast_in_dim.5), channel_id=1, replica_groups=mesh['z'=12,'y_hi'=2,'x'=4,'core'=2,'slab'=4] {'x','core'}, dimensions={0} | all-to-all | bytes 8192 | tf_op jit(solution)/shard_map/all_to_all | solution.py:209
  104.6 0.5 shard_map.38
  105.1 0.0 collective-permute-done.5.recv_b_ref
  105.1 0.0 collective-permute-done.4.recv_a_ref
  105.1 0.0 copy-done.1
  105.1 5.0 %shard_map.37 = bf16[1,896,1024]{2,1,0:T(8,128)(2,1)} custom-call(s32[1]{0:T(128)} %bitcast.own_ref, bf16[784,256]{1,0:T(8,128)(2,1)S(1)} %shard_map.33.keep_a_ref, bf16[272,256]{1,0:T(8,128)(2,1)S(1)} %shard_map.36.keep_b_ref, bf16[784,256]{1,0:T(8,128)(2,1)S(1)} %collective-permute-done.4.recv_a_ref, ...), custom_call_target="tpu_custom_call" | custom-call | flops 3758096384 | bytes 3670016 | tf_op jit(solution)/shard_map/pallas_call | solution.py:179
  (6 shorter events, 0.1 us)
Async XLA Ops:
  0.6 1.5 %copy-start = (bf16[1,896,1024]{2,1,0:T(8,128)(2,1)S(1)}, bf16[1,896,1024]{2,1,0:T(8,128)(2,1)}, u32[]{:S(2)}) copy-start(bf16[1,896,1024]{2,1,0:T(8,128)(2,1)} %x_ref.7) | copy-start | bytes 5505028
  2.9 9.3 %collective-permute-start = (bf16[784,256]{1,0:T(8,128)(2,1)S(1)}, bf16[784,256]{1,0:T(8,128)(2,1)S(1)}, u32[]{:S(2)}, u32[]{:S(2)}) collective-permute-start(bf16[784,256]{1,0:T(8,128)(2,1)S(1)} %shard_map.31), channel_id=1, source_target_pairs={{0,1},{1,0},{2,3},{3,2},{4,5},{5,4},{6,7},{7,6},{8,9},{9,8},{10,11... | collective-permute-start | bytes 1204232 | tf_op jit(solution)/shard_map/ppermute | solution.py:222
  12.3 92.8 %copy-start.1 = (bf16[1,896,1024]{2,1,0:T(8,128)(2,1)S(1)}, bf16[1,896,1024]{2,1,0:T(8,128)(2,1)}, u32[]{:S(2)}) copy-start(bf16[1,896,1024]{2,1,0:T(8,128)(2,1)} %x_ref.7) | copy-start | bytes 5505028
  12.3 14.3 %collective-permute-start.1 = (bf16[784,256]{1,0:T(8,128)(2,1)S(1)}, bf16[784,256]{1,0:T(8,128)(2,1)S(1)}, u32[]{:S(2)}, u32[]{:S(2)}) collective-permute-start(bf16[784,256]{1,0:T(8,128)(2,1)S(1)} %shard_map.32.a_ref), channel_id=1, source_target_pairs={{1,2},{2,1},{0,3},{3,0},{5,6},{6,5},{4,7},{7,4},{9,10},{10,9},{8,1... | collective-permute-start | bytes 1204232 | tf_op jit(solution)/shard_map/ppermute | solution.py:227
  21.7 12.9 %collective-permute-start.2 = (bf16[272,256]{1,0:T(8,128)(2,1)S(1)}, bf16[272,256]{1,0:T(8,128)(2,1)S(1)}, u32[]{:S(2)}, u32[]{:S(2)}) collective-permute-start(bf16[272,256]{1,0:T(8,128)(2,1)S(1)} %get-tuple-element.8), channel_id=1, source_target_pairs={{0,1},{1,0},{2,3},{3,2},{4,5},{5,4},{6,7},{7,6},{8,9},{9,8},{10,11... | collective-permute-start | bytes 417800 | tf_op jit(solution)/shard_map/ppermute | solution.py:224
  26.7 78.4 %collective-permute-start.4 = (bf16[784,256]{1,0:T(8,128)(2,1)S(1)}, bf16[784,256]{1,0:T(8,128)(2,1)S(1)}, u32[]{:S(2)}, u32[]{:S(2)}) collective-permute-start(bf16[784,256]{1,0:T(8,128)(2,1)S(1)} %shard_map.33.keep_a_ref), channel_id=1, source_target_pairs={{0,1},{1,0},{2,3},{3,2},{4,5},{5,4},{6,7},{7,6},{8,9},{9,8},{10,11... | collective-permute-start | bytes 1204232 | tf_op jit(solution)/shard_map/ppermute | solution.py:233
  34.7 16.3 %collective-permute-start.3 = (bf16[272,256]{1,0:T(8,128)(2,1)S(1)}, bf16[272,256]{1,0:T(8,128)(2,1)S(1)}, u32[]{:S(2)}, u32[]{:S(2)}) collective-permute-start(bf16[272,256]{1,0:T(8,128)(2,1)S(1)} %shard_map.35.a_ref), channel_id=1, source_target_pairs={{1,2},{2,1},{0,3},{3,0},{5,6},{6,5},{4,7},{7,4},{9,10},{10,9},{8,1... | collective-permute-start | bytes 417800 | tf_op jit(solution)/shard_map/ppermute | solution.py:231
  51.0 54.2 %collective-permute-start.5 = (bf16[272,256]{1,0:T(8,128)(2,1)S(1)}, bf16[272,256]{1,0:T(8,128)(2,1)S(1)}, u32[]{:S(2)}, u32[]{:S(2)}) collective-permute-start(bf16[272,256]{1,0:T(8,128)(2,1)S(1)} %shard_map.36.keep_b_ref), channel_id=1, source_target_pairs={{0,1},{1,0},{2,3},{3,2},{4,5},{5,4},{6,7},{7,6},{8,9},{9,8},{10,11... | collective-permute-start | bytes 417800 | tf_op jit(solution)/shard_map/ppermute | solution.py:235
